TPU v7x, 32 devices: a whole 2x2x4 slice. The times are simulated.
32 devices in a mesh: groups: 2 (over x), tm: 16 (over z, y, core).
Axes of the slice: x: 2, y: 2, z: 4, core: 2. Of those that a mesh axis runs over, the one named last changes fastest.
Arguments:
- receptance: bfloat16 [4096, 1024], P(('groups', 'tm')), parts along dimension 0, may hold values from -0.75 to 0.75
- key_input: bfloat16 [4096, 1024], P(('groups', 'tm')), parts along dimension 0, may hold values from -6 to 6
- values: bfloat16 [4096, 1024], P(('groups', 'tm')), parts along dimension 0, may hold values from -6 to 6
- log_decay: bfloat16 [4096, 1024], P(('groups', 'tm')), parts along dimension 0, may hold values from -1 to 0
- kappa_raw: bfloat16 [4096, 1024], P(('groups', 'tm')), parts along dimension 0, may hold values from -6 to 6
- removal: bfloat16 [4096, 1024], P(('groups', 'tm')), parts along dimension 0, may hold values from 0 to 1
- initial_state: float32 [32, 64, 64], P('groups'), parts along dimension 0, may hold values from -3 to 3
- out_weight: bfloat16 [1024, 1024], replicated, may hold values from -0.1875 to 0.1875
- grad_output: bfloat16 [1024, 4096], P('tm', 'groups'), parts along dimension 1, may hold values from -6 to 6
Outputs:
- grad_receptance: bfloat16 [4096, 1024], P(('groups', 'tm')), parts along dimension 0
- grad_keys: bfloat16 [4096, 1024], P(('groups', 'tm')), parts along dimension 0
- grad_values: bfloat16 [4096, 1024], P(('groups', 'tm')), parts along dimension 0
- grad_weight: float32 [2048, 1024], P(('groups', 'tm')), parts along dimension 0
There are 2 independent parts, one for each index of `groups`. A program takes and returns all parts, laid end to end along the dimension named above; an argument that names none is the same for every part. Nothing has to cross between parts.
All inputs are finite; a program needn't handle non-finite values.
Results may differ from a plain program's by a relative error of at most 0.0029.
Values may be sent and summed in bfloat16 or wider, within the bound.
A program may use at most 320 MiB of HBM per device.

v0:
```python
import math

import jax
import jax.numpy as jnp
from jax import lax
from jax.sharding import PartitionSpec as P

HEAD_COUNT = 16
HEAD_SIZE = 64


def prefix(x, axis, combine, identity):
    size, position = (lax.axis_size(axis), lax.axis_index(axis))
    everything = jax.tree.map(lambda part: lax.all_gather(part, axis), x)
    start = jax.tree.map(
        lambda part, zero: jnp.broadcast_to(jnp.asarray(zero, part.dtype), part.shape), x, identity
    )

    def lap(k, before):
        reached = k < position
        new = combine(before, jax.tree.map(lambda part: part[k], everything))
        return jax.tree.map(lambda a, b: jnp.where(reached, a, b), new, before)

    return lax.fori_loop(0, size, lap, start)


def shifted(x, axis, by):
    size = lax.axis_size(axis)
    pairs = [(i, i + by) for i in range(size) if 0 <= i + by < size]
    return lax.ppermute(x, axis, pairs)


def make_frames(receptance, key_input, values, log_decay, kappa_raw, removal, grad_y):
    frame_count = receptance.shape[0]
    head_shape = (frame_count, HEAD_COUNT, HEAD_SIZE)
    log_part = log_decay.astype(jnp.float32).reshape(head_shape)
    decays = jnp.exp(log_part)
    key_scale = jnp.sqrt(-jnp.expm1(log_part))
    raw_key = kappa_raw.astype(jnp.float32).reshape(head_shape)
    unit_key = raw_key / jnp.sqrt(jnp.sum(raw_key * raw_key, -1, keepdims=True) + 1e-06)
    gated_key = removal.astype(jnp.float32).reshape(head_shape) * unit_key
    keys_in = key_input.astype(jnp.float32).reshape(head_shape) * key_scale
    value_rows = values.astype(jnp.float32).reshape(head_shape)
    recept_rows = receptance.astype(jnp.float32).reshape(head_shape)
    grad_rows = grad_y.reshape(head_shape)
    return (decays, unit_key, gated_key, value_rows, keys_in, recept_rows, grad_rows, key_scale)


def advance(current, decays, unit_key, gated_key, value_rows, keys_in):
    projected = jnp.sum(current * unit_key[..., None, :], -1)
    return (
        current * decays[..., None, :]
        - projected[..., :, None] * gated_key[..., None, :]
        + value_rows[..., :, None] * keys_in[..., None, :]
    )


def pull_back(grad_state, decays, unit_key, gated_key):
    pulled = jnp.sum(grad_state * gated_key[..., None, :], -1)
    return grad_state * decays[..., None, :] - pulled[..., :, None] * unit_key[..., None, :]


def forward_step(current, frame_slice):
    decays, unit_key, gated_key, value_rows, keys_in, recept_rows, grad_rows, key_scale = (
        frame_slice
    )
    current = advance(current, decays, unit_key, gated_key, value_rows, keys_in)
    out_y = jnp.sum(current * recept_rows[:, None, :], -1)
    grad_r = jnp.sum(current * grad_rows[:, :, None], -2)
    return (current, (out_y, grad_r))


def transition_step(current, frame_slice):
    decays, unit_key, gated_key, value_rows, keys_in, recept_rows, grad_rows, key_scale = (
        frame_slice
    )
    selector = jnp.array([1.0, 0.0], jnp.float32)[:, None, None]
    return (advance(current, decays, unit_key, gated_key, value_rows[None] * selector, keys_in), ())


def backward_step(incoming, frame_slice):
    decays, unit_key, gated_key, value_rows, keys_in, recept_rows, grad_rows, key_scale = (
        frame_slice
    )
    grad_state = incoming + grad_rows[:, :, None] * recept_rows[:, None, :]
    grad_v = jnp.sum(grad_state * keys_in[:, None, :], -1)
    grad_k = jnp.sum(grad_state * value_rows[:, :, None], -2) * key_scale
    return (pull_back(grad_state, decays, unit_key, gated_key), (grad_v, grad_k))


def pull_step(incoming, frame_slice):
    decays, unit_key, gated_key, value_rows, keys_in, recept_rows, grad_rows, key_scale = (
        frame_slice
    )
    grad_state = incoming + grad_rows[:, :, None] * recept_rows[:, None, :]
    return (pull_back(grad_state, decays, unit_key, gated_key), ())


def blockwise(step_fn, carried, arrays, block_len, backwards):
    frame_count = arrays[0].shape[0]
    blocked = tuple(
        (
            array_in.reshape((frame_count // block_len, block_len) + array_in.shape[1:])
            for array_in in arrays
        )
    )

    def visit(current, block_data):
        outputs = []
        if backwards:
            sequence_order = range(block_len - 1, -1, -1)
        else:
            sequence_order = range(block_len)
        for position in sequence_order:
            current, result = step_fn(current, tuple((member[position] for member in block_data)))
            outputs.append(result)
        if backwards:
            outputs = outputs[::-1]
        stacked = jax.tree.map(lambda *leaves: jnp.stack(leaves), *outputs)
        return (current, stacked)

    carried, results = lax.scan(visit, carried, blocked, reverse=backwards)
    results = jax.tree.map(
        lambda array_in: array_in.reshape((frame_count,) + array_in.shape[2:]), results
    )
    return (carried, results)


def matmul_heads(left_mat, right_mat):
    return jnp.einsum("hij,hjk->hik", left_mat, right_mat, precision=lax.Precision.HIGHEST)


def compose_forward(earlier_pair, later_pair):
    return (
        matmul_heads(earlier_pair[0], later_pair[0]),
        matmul_heads(earlier_pair[1], later_pair[0]) + later_pair[1],
    )


def local(
    receptance,
    key_input,
    values,
    log_decay,
    kappa_raw,
    removal,
    initial_state,
    out_weight,
    grad_output,
):
    gathered = lax.all_to_all(grad_output, "tm", split_axis=1, concat_axis=0, tiled=True)
    grad_y = lax.dot_general(
        gathered, out_weight, (((0,), (1,)), ((), ())), preferred_element_type=jnp.float32
    )
    frames = make_frames(receptance, key_input, values, log_decay, kappa_raw, removal, grad_y)
    frame_count = receptance.shape[0]
    block_len = math.gcd(frame_count, 32)
    identity_mat = jnp.broadcast_to(
        jnp.eye(HEAD_SIZE, dtype=jnp.float32), (HEAD_COUNT, HEAD_SIZE, HEAD_SIZE)
    )
    zero_state = jnp.zeros((HEAD_COUNT, HEAD_SIZE, HEAD_SIZE), jnp.float32)
    transfer_pair, _ = blockwise(
        transition_step, jnp.stack([zero_state, identity_mat]), frames, block_len, False
    )
    offset, through = (transfer_pair[0], transfer_pair[1])
    local_pull, _ = blockwise(pull_step, zero_state, frames, block_len, True)
    passed = jnp.swapaxes(through, -1, -2)
    prior = prefix((through, offset), "tm", compose_forward, (identity_mat, zero_state))
    entry_state = matmul_heads(initial_state, prior[0]) + prior[1]

    def relay(step_number, grad_in):
        grad_out = local_pull + matmul_heads(grad_in, passed)
        return shifted(grad_out, "tm", -1)

    entry_grad = lax.fori_loop(0, lax.axis_size("tm") - 1, relay, zero_state)
    _, (out_y, grad_r) = blockwise(forward_step, entry_state, frames, block_len, False)
    _, (grad_v, grad_k) = blockwise(backward_step, entry_grad, frames, block_len, True)
    flat_shape = (frame_count, HEAD_COUNT * HEAD_SIZE)
    y_low = out_y.reshape(flat_shape).astype(jnp.bfloat16)
    loss_scale = 1.0 / math.sqrt(frame_count * lax.axis_size("tm"))
    grad_weight = lax.psum_scatter(
        lax.dot_general(
            y_low, gathered, (((0,), (1,)), ((), ())), preferred_element_type=jnp.float32
        )
        * loss_scale,
        "tm",
        scatter_dimension=0,
        tiled=True,
    )
    return (
        grad_r.reshape(flat_shape).astype(jnp.bfloat16),
        grad_k.reshape(flat_shape).astype(jnp.bfloat16),
        grad_v.reshape(flat_shape).astype(jnp.bfloat16),
        grad_weight,
    )


def solution(mesh):
    return jax.shard_map(
        local,
        mesh=mesh,
        in_specs=(
            P(("groups", "tm"), None),
            P(("groups", "tm"), None),
            P(("groups", "tm"), None),
            P(("groups", "tm"), None),
            P(("groups", "tm"), None),
            P(("groups", "tm"), None),
            P("groups", None, None),
            P(),
            P("tm", "groups"),
        ),
        out_specs=(
            P(("groups", "tm"), None),
            P(("groups", "tm"), None),
            P(("groups", "tm"), None),
            P(("groups", "tm"), None),
        ),
        check_vma=False,
    )
```

profile of v0, /device:TPU:0, one launch (start us, length us, event | category | flops | bytes accessed | tf_op | source)
XLA Modules:
  0.0 2405.4 jit_solution(11145872064270799366)
XLA Ops:
  25.5 546.5 %while.88 = (s32[]{:T(128)}, f32[2,16,64,64]{3,2,1,0:T(8,128)S(1)}, f32[4,32,16,64]{3,2,1,0:T(8,128)}, f32[4,32,16,64]{3,2,1,0:T(8,128)}, f32[4,32,16,64]{3,2,1,...) while((s32[]{:T(128)}, f32[2,16,64,64]{3,2,1,0:T(8,128)S(1)}, ...), condition=%wide.region_34.35_spmd.clone.clone, body=%wide.region_1.34_spmd.sunk.clone.clone.sunk | while | flops 25298952 | bytes 36046076 | solution.py:122
  42.9 4.0 fusion.1890
  46.9 4.0 fusion.1891
  574.1 7.4 all-to-all-start
  587.0 6.6 all-to-all-done
  598.1 349.9 %while.90 = (s32[]{:T(128)}, f32[16,64,64]{2,1,0:T(8,128)}, f32[4,32,16,64]{3,2,1,0:T(8,128)}, f32[4,32,16,64]{3,2,1,0:T(8,128)}, f32[4,32,16,64]{3,2,1,0:T(8,12...) while((s32[]{:T(128)}, f32[16,64,64]{2,1,0:T(8,128)}, ...), condition=%wide.region_168.169_spmd.clone, body=%wide.region_135.168_spmd.clone.sunk | while | flops 12879875 | bytes 18744580 | solution.py:122
  601.0 4.9 fusion.1961
  688.5 5.1 fusion.1961
  776.0 5.1 fusion.1961
  863.5 5.1 fusion.1961
  948.1 117.0 %while.89 = (s32[]{:T(128)}, f32[16,64,64]{1,2,0:T(8,128)S(1)}, f32[16,64,64]{1,2,0:T(8,128)}, s32[]{:T(128)}, f32[16,16,64,64]{3,2,1,0:T(8,128)}, /*index=5*/f32[16,16,64,64]{3,2,1,0:T(8,128)}, s32[]{:T(128)}, s32[]{:T(128)}) while((s32[]{:T(128)}, f32[16,64,64]{1,2,0:T(8,128)S(1)}, f32[16,64,64]{1,2,0:T(8,128)}, s32[]{:T(128)}, ...), condition=%wide.region_36.0_spmd.clone, body=%wide.region_35.36_spmd.clone.sunk | while | flops 100990976 | bytes 6294124 | solution.py:24
  1069.3 529.8 %while.85 = (s32[]{:T(128)}, f32[16,64,64]{2,1,0:T(8,128)}, bf16[4,32,16,64]{3,2,1,0:T(8,128)(2,1)S(1)}, bf16[4,32,16,64]{3,2,1,0:T(8,128)(2,1)}, f32[4,32,16,64...) while((s32[]{:T(128)}, f32[16,64,64]{2,1,0:T(8,128)}, ...), condition=%wide.region_134.135_spmd, body=%wide.region_37.134_spmd.sunk | while | flops 20940804 | bytes 21503456 | solution.py:122
  1078.9 4.6 multiply_reduce_fusion.320
  1142.4 4.2 multiply_reduce_fusion.336
  1146.7 4.2 multiply_reduce_fusion.337
  1151.0 4.2 multiply_reduce_fusion.338
  1211.3 4.6 multiply_reduce_fusion.320
  1274.8 4.2 multiply_reduce_fusion.336
  1279.1 4.2 multiply_reduce_fusion.337
  1283.4 4.2 multiply_reduce_fusion.338
  1343.7 4.6 multiply_reduce_fusion.320
  1407.2 4.2 multiply_reduce_fusion.336
  1411.5 4.2 multiply_reduce_fusion.337
  1415.8 4.2 multiply_reduce_fusion.338
  1476.0 4.6 multiply_reduce_fusion.320
  1539.6 4.2 multiply_reduce_fusion.336
  1543.9 4.2 multiply_reduce_fusion.337
  1548.2 4.2 multiply_reduce_fusion.338
  1602.2 206.9 %while.86 = (s32[]{:T(128)}, f32[16,64,64]{2,1,0:T(8,128)S(1)}, f32[16,64,64]{2,1,0:T(8,128)S(1)}, f32[16,64,64]{2,1,0:T(8,128)}, s32[]{:T(128)}) while((s32[]{:T(128)}, f32[16,64,64]{2,1,0:T(8,128)S(1)}, f32[16,64,64]{2,1,0:T(8,128)S(1)}, f32[16,64,64]{2,1,0:T(8,128)}, s32[]{:T(128)}) %tuple.1360), condition=%wide.region_170.171_spmd, body=%wide.region_169.170_spmd.sunk | while | flops 50397184 | bytes 2097253 | solution.py:175
  1612.6 9.1 collective-permute-done
  1625.5 9.2 collective-permute-done
  1638.5 20.0 collective-permute-done
  1662.4 9.4 collective-permute-done
  1675.5 9.4 collective-permute-done
  1688.8 9.4 collective-permute-done
  1702.0 9.4 collective-permute-done
  1715.1 9.4 collective-permute-done
  1728.3 10.3 collective-permute-done
  1742.4 10.3 collective-permute-done
  1756.5 10.3 collective-permute-done
  1770.6 10.3 collective-permute-done
  1784.7 10.3 collective-permute-done
  1798.8 10.3 collective-permute-done
  1810.8 581.0 %while.87 = (s32[]{:T(128)}, f32[16,64,64]{2,1,0:T(8,128)S(1)}, bf16[4,32,16,64]{3,2,1,0:T(8,128)(2,1)}, bf16[4,32,16,64]{3,2,1,0:T(8,128)(2,1)}, f32[4,32,16,64...) while((s32[]{:T(128)}, f32[16,64,64]{2,1,0:T(8,128)S(1)}, ...), condition=%wide.region_268.269_spmd, body=%wide.region_171.268_spmd.sunk | while | flops 21235720 | bytes 21303200 | solution.py:122
  1816.0 4.5 multiply_reduce_fusion.352
  1961.2 4.5 multiply_reduce_fusion.352
  2106.4 4.5 multiply_reduce_fusion.352
  2251.6 4.5 multiply_reduce_fusion.352
  (1788 shorter events, 2103.8 us)
Async XLA Ops:
  7.2 587.3 %copy-start = (bf16[1024,1024]{1,0:T(8,128)(2,1)S(1)}, bf16[1024,1024]{1,0:T(8,128)(2,1)}, u32[]{:S(2)}) copy-start(bf16[1024,1024]{1,0:T(8,128)(2,1)} %param.60) | copy-start | bytes 6291460
  7.2 940.8 %all-gather.3.cloned.1.call-start = ((), (), s32[]{:S(2)}) async-start(), calls=%async_computation.2 | async-start | bytes 8912896 | tf_op jit(solution)/shard_map/all_gather | solution.py:14
  25.5 547.8 %copy-start.12 = (bf16[64,2048]{1,0:T(8,128)(2,1)S(1)}, bf16[64,2048]{1,0:T(8,128)(2,1)}, u32[]{:S(2)}) copy-start(bf16[64,2048]{1,0:T(8,128)(2,1)} %param.61) | copy-start | bytes 786436
  574.1 19.5 all-to-all-start
  581.5 366.5 %all-gather.5.cloned.1.call-start = ((), (), s32[]{:S(2)}) async-start(), calls=%async_computation.3 | async-start | bytes 8912896 | tf_op jit(solution)/shard_map/all_gather | solution.py:14
  582.2 1816.2 %reduce-scatter.2.cloned.1.call-start = ((), (), s32[]{:S(2)}) async-start(), calls=%async_computation.4 | async-start | bytes 4456448 | tf_op jit(solution)/shard_map/reduce_scatter | solution.py:181
  598.1 349.9 %copy-start.9 = (f32[64,64]{0,1:T(8,128)S(1)}, f32[64,64]{0,1:T(8,128)}, u32[]{:S(2)}) copy-start(f32[64,64]{0,1:T(8,128)} %copy-done.8) | copy-start | bytes 49156
  1131.5 23.8 copy-start.16
  1131.5 23.8 copy-start.25
  1131.5 23.8 copy-start.34
  1131.5 23.8 copy-start.42
  1131.5 23.8 copy-start.49
  1135.1 23.8 copy-start.18
  1135.1 23.8 copy-start.27
  1135.1 23.8 copy-start.36
  1135.1 23.8 copy-start.44
  1135.1 23.8 copy-start.51
  1263.8 23.8 copy-start.16
  1267.4 23.8 copy-start.18
  1267.4 23.8 copy-start.27
  1267.5 23.8 copy-start.36
  1267.5 23.8 copy-start.44
  1267.5 23.8 copy-start.51
  1399.8 23.8 copy-start.18
  1399.8 23.8 copy-start.27
  1399.8 23.8 copy-start.36
  1399.8 23.8 copy-start.44
  1399.9 23.8 copy-start.51
  1532.2 23.8 copy-start.18
  1532.2 23.8 copy-start.27
  1532.2 23.8 copy-start.36
  1532.2 23.8 copy-start.44
  1532.2 23.8 copy-start.51
  1604.7 4.0 collective-permute-start
  1611.3 10.4 collective-permute-start
  1624.2 10.5 collective-permute-start
  1637.2 21.3 collective-permute-start
  1661.1 10.7 collective-permute-start
  1674.2 10.7 collective-permute-start
  1687.5 10.7 collective-permute-start
  1700.7 10.7 collective-permute-start
  1713.9 10.7 collective-permute-start
  1727.0 11.6 collective-permute-start
  1741.1 11.6 collective-permute-start
  1755.2 11.6 collective-permute-start
  1769.3 11.6 collective-permute-start
  1783.4 11.6 collective-permute-start
  1797.5 11.6 collective-permute-start
  (180 other events, 3869.5 us)
Sparse Core Ops, SparseCore 0:
  573.4 79.9 all-gather.2
  655.6 72.9 all-gather.4
  1602.3 82.1 reduce-scatter.1
where the time goes:
time: 2450 us; the launch traced here: 2410 us
  other arithmetic  1840 us (75%)
  local copies, waits for them, and re-layouts  238 us (10%)
  waiting for transfers between devices  157 us (6%)
  matrix products  123 us (5%)
  starting transfers between devices  26.9 us (1%)
    mul x256, other arithmetic, advance(): projected[..., :, None] * gated_key[..., None, :]  967 us
    mul x256, other arithmetic, pull_back(): pulled[..., :, None] * unit_key[..., None, :]  764 us
    ppermute x15, waiting for transfers between devices, shifted(): return lax.ppermute(x, axis, pairs)  150 us
    dot_general x48, matrix products, matmul_heads(): jnp.einsum('hij,hjk->hik', left_mat, right_mat, precision=lax.Precision.H...  118 us
    while x124, other arithmetic  87.5 us
  transfers between devices with their start and end apart: 19, of which 16 were waited for; matrix products, arithmetic and copies ran while one was open for 41% of the time, Pallas kernels for 0%

commit v1 on v0

v1 whole, which is shorter than its diff:
```python
import functools
import math

import jax
import jax.numpy as jnp
from jax import lax
from jax.experimental import pallas as pl
from jax.experimental.pallas import tpu as pltpu
from jax.sharding import PartitionSpec as P

HEAD_COUNT = 16
HEAD_SIZE = 64
PAIR = 2 * HEAD_SIZE
PAIRS = HEAD_COUNT // 2
F32 = jnp.float32
BF16 = jnp.bfloat16

NN = (((1,), (0,)), ((), ()))
NT = (((1,), (1,)), ((), ()))
TN = (((0,), (0,)), ((), ()))


def split(x):
    high = x.astype(BF16)
    return high, (x - high.astype(F32)).astype(BF16)


def dot1(a, b, dims):
    return lax.dot_general(a, b, dims, preferred_element_type=F32)


def dot3(a, b, dims):
    a = (a,) if not isinstance(a, tuple) and a.dtype == BF16 else a if isinstance(a, tuple) else split(a)
    b = (b,) if not isinstance(b, tuple) and b.dtype == BF16 else b if isinstance(b, tuple) else split(b)
    out = dot1(a[0], b[0], dims)
    if len(b) > 1:
        out = out + dot1(a[0], b[1], dims)
    if len(a) > 1:
        out = out + dot1(a[1], b[0], dims)
    return out


def iota(shape, dim):
    return lax.broadcasted_iota(jnp.int32, shape, dim)


def both(f, lane_low):
    return jnp.where(lane_low, f(0), f(1))


def pack(full, lane_low):
    return jnp.where(lane_low, full[:HEAD_SIZE], full[HEAD_SIZE:])


def unpack(packed, diagonal):
    return jnp.where(diagonal, jnp.concatenate([packed, packed], 0), 0.0)


def inverses(lower, row, col):
    size = row.shape[0]
    eye = jnp.where(row == col, 1.0, 0.0).astype(F32)
    step = 1
    out = None
    while step < size:
        inside = (row // (2 * step) == col // (2 * step)) & (row // step != col // step)
        off = [jnp.where(inside, m, 0.0) for m in lower]
        if out is None:
            out = [eye - m for m in off]
        else:
            halves = [split(t) for t in out]
            mid = [dot3(m, t, NN) for m, t in zip(off, halves)]
            out = [t - dot3(h, m, NN) for t, h, m in zip(out, halves, mid)]
        step *= 2
    return out


SAVED = 14


def one_less_exp(x):
    series = jnp.full_like(x, 1.0 / math.factorial(10))
    for n in range(9, 0, -1):
        series = series * x + 1.0 / math.factorial(n)
    return jnp.where(x > -0.5, -x * series, 1.0 - jnp.exp(x))


def first_kernel(rows_each, rec_ref, key_ref, val_ref, log_ref, kap_ref, rem_ref, gy_ref, pay_ref, *saved):
    frames = rec_ref.shape[0]
    row, col = iota((frames, frames), 0), iota((frames, frames), 1)
    lane_low = iota((frames, PAIR), 1) < HEAD_SIZE
    pack_low = iota((HEAD_SIZE, PAIR), 1) < HEAD_SIZE
    prow, pcol = iota((PAIR, PAIR), 0), iota((PAIR, PAIR), 1)
    diagonal = (prow // HEAD_SIZE) == (pcol // HEAD_SIZE)
    ones = jnp.where(diagonal, 1.0, 0.0).astype(BF16)
    tri = jnp.where(row >= col, 1.0, 0.0).astype(BF16)
    own = [lane_low, jnp.logical_not(lane_low)]

    count = rec_ref.shape[1] // PAIR
    for pair in range(count):
        at = pl.ds(pair * PAIR, PAIR)
        log_low = log_ref[:, at]
        log_part = log_low.astype(F32)
        total = dot1(tri, log_low, NN)
        middle, last = total[frames // 2 - 1 : frames // 2], total[frames - 1 : frames]
        key_scale = jnp.sqrt(one_less_exp(log_part))
        raw = kap_ref[:, at].astype(F32)
        norm = dot3(raw * raw, ones, NN)
        a = raw / jnp.sqrt(norm + 1e-06)
        b = rem_ref[:, at].astype(F32) * a
        k = key_ref[:, at].astype(F32) * key_scale
        r = rec_ref[:, at].astype(F32)
        v = val_ref[:, at]
        q = split(gy_ref[:, at])
        e_pos, e_prev, e_neg = (
            jnp.exp(total - middle), jnp.exp(total - log_part - middle), jnp.exp(middle - total)
        )
        e_abs, e_end = jnp.exp(total), jnp.exp(last - total)
        a_mid, r_mid, b_mid, k_mid = a * e_prev, r * e_pos, b * e_neg, k * e_neg
        a_abs, r_abs = a * jnp.exp(total - log_part), r * e_abs
        b_end, k_end = b * e_end, k * e_end

        upper = split(jnp.concatenate([a_mid, r_mid], 0))
        rights = split(jnp.concatenate([b_mid, k_mid], 0))
        own2 = [jnp.concatenate([m, m], 0) for m in own]
        zero = jnp.zeros((), BF16)
        grams = [dot3(upper, tuple(jnp.where(m, x, zero) for x in rights), NT) for m in own2]
        strict, lax_tri = row > col, row >= col
        m_ab = [jnp.where(strict, g[:frames, :frames], 0.0) for g in grams]
        m_ak = [jnp.where(strict, g[:frames, frames:], 0.0) for g in grams]
        m_rb = [split(jnp.where(lax_tri, g[frames:, :frames], 0.0)) for g in grams]
        m_rk = [split(jnp.where(lax_tri, g[frames:, frames:], 0.0)) for g in grams]
        t_inv = [split(t) for t in inverses(m_ab, row, col)]
        m_ak = [split(m) for m in m_ak]

        low2 = jnp.concatenate([lane_low, lane_low], 1)
        start = both(lambda h: dot3(m_ak[h], v, NN), lane_low)
        first = split(jnp.concatenate([start, a_abs], 1))
        inner = both(lambda h: dot3(t_inv[h], first, NN), low2)
        u0, x = inner[:, :PAIR], inner[:, PAIR:]
        inner = split(inner)
        minus = both(lambda h: dot3(m_rb[h], inner, NN), low2)
        y0 = both(lambda h: dot3(m_rk[h], v, NN), lane_low) - minus[:, :PAIR]
        yr = r_abs - minus[:, PAIR:]

        back = both(lambda h: dot3(m_rb[h], q, TN), lane_low)
        second = split(jnp.concatenate([back, b_end], 1))
        pulled = both(lambda h: dot3(t_inv[h], second, TN), low2)
        p0, tb = pulled[:, :PAIR], pulled[:, PAIR:]
        pulled = split(pulled)
        minus = both(lambda h: dot3(m_ak[h], pulled, TN), low2)
        gv0 = both(lambda h: dot3(m_rk[h], q, TN), lane_low) - minus[:, :PAIR]
        gvk = k_end - minus[:, PAIR:]

        v_own = [jnp.where(m, v, zero) for m in own]
        q_own = [tuple(jnp.where(m, x_, zero) for x_ in q) for m in own]
        k_mid_s, r_mid_s = split(k_mid), split(r_mid)
        gra = e_pos * both(
            lambda h: dot3(jnp.where(lax_tri, dot3(q, v_own[h], NT), 0.0), k_mid_s, NN), lane_low
        )
        gka = e_neg * both(
            lambda h: dot3(jnp.where(row <= col, dot3(v, q_own[h], NT), 0.0), r_mid_s, NN), lane_low
        )

        b_end_s = split(b_end)
        both_end = dot3(inner, b_end_s, TN)
        ends = jnp.where(prow == pcol, jnp.exp(last), 0.0) - both_end[PAIR:]
        offset = dot3(v, k_end, TN) - both_end[:PAIR]
        pull = dot3(q, r_abs, TN) - dot3(p0, a_abs, TN)
        through, offset, pull = pack(ends, pack_low), pack(offset, pack_low), pack(pull, pack_low)
        for part in range(HEAD_SIZE // rows_each):
            rows = slice(part * rows_each, (part + 1) * rows_each)
            to = pair * (HEAD_SIZE // rows_each) + part
            pay_ref[to, :HEAD_SIZE] = through
            pay_ref[to, HEAD_SIZE : HEAD_SIZE + rows_each] = offset[rows]
            pay_ref[to, HEAD_SIZE + rows_each :] = pull[rows]

        keep = (u0, x, y0, yr, p0, tb, gv0, gvk, gra, gka * key_scale,
                total, b_mid, a_mid, key_scale)
        for ref, value in zip(saved, keep):
            ref[:, at] = value


def relay_kernel(rows_each, pay_ref, start_ref, out_ref):
    count = pay_ref.shape[0]
    diagonal = (iota((PAIR, PAIR), 0) // HEAD_SIZE) == (iota((PAIR, PAIR), 1) // HEAD_SIZE)

    def lap(i, carried):
        state, grad = carried
        j = count - 1 - i
        out_ref[i, :rows_each] = state
        out_ref[j, rows_each:] = grad
        state = pay_ref[i, HEAD_SIZE : HEAD_SIZE + rows_each] + dot3(
            state, unpack(pay_ref[i, :HEAD_SIZE], diagonal), NN
        )
        grad = pay_ref[j, HEAD_SIZE + rows_each :] + dot3(
            grad, unpack(pay_ref[j, :HEAD_SIZE], diagonal), NT
        )
        return state, grad

    lax.fori_loop(0, count, lap, (start_ref[...], jnp.zeros((rows_each, PAIR), F32)))


def last_kernel(state_ref, grad_ref, gy_ref, val_ref, u_ref, x_ref, y_ref, yr_ref, p_ref, tb_ref,
                gv_ref, gvk_ref, gra_ref, gka_ref, tot_ref, b_ref, a_ref, ks_ref,
                ylow_ref, gr_out, gk_out, gv_out):
    frames = gy_ref.shape[0]
    row, col = iota((frames, frames), 0), iota((frames, frames), 1)
    lane_low = iota((frames, PAIR), 1) < HEAD_SIZE
    own = [lane_low, jnp.logical_not(lane_low)]
    diagonal = (iota((PAIR, PAIR), 0) // HEAD_SIZE) == (iota((PAIR, PAIR), 1) // HEAD_SIZE)
    zero = jnp.zeros((), BF16)
    for pair in range(gy_ref.shape[1] // PAIR):
        at = pl.ds(pair * PAIR, PAIR)
        state = split(unpack(state_ref[pair], diagonal))
        grad = split(unpack(grad_ref[pair], diagonal))
        q, v = split(gy_ref[:, at]), val_ref[:, at]
        ahead = dot3(jnp.concatenate([x_ref[:, at], yr_ref[:, at]], 0), state, NT)
        u = split(u_ref[:, at] + ahead[:frames])
        ylow_ref[:, at] = (y_ref[:, at] + ahead[frames:]).astype(BF16)
        behind = dot3(jnp.concatenate([tb_ref[:, at], gvk_ref[:, at]], 0), grad, NT)
        p = split(p_ref[:, at] + behind[:frames])
        gv_out[:, at] = (gv_ref[:, at] + behind[frames:]).astype(BF16)
        b_mid, a_mid = split(b_ref[:, at]), split(a_ref[:, at])
        total = tot_ref[:, at]
        middle, last = total[frames // 2 - 1 : frames // 2], total[frames - 1 : frames]

        def removed(h):
            gram = dot3(q, tuple(jnp.where(own[h], x, zero) for x in u), NT)
            return dot3(jnp.where(row >= col, gram, 0.0), b_mid, NN)

        def removed_back(h):
            gram = dot3(v, tuple(jnp.where(own[h], x, zero) for x in p), NT)
            return dot3(jnp.where(row < col, gram, 0.0), a_mid, NN)

        gr = jnp.exp(total) * dot3(q, state, NN) + gra_ref[:, at]
        gr = gr - jnp.exp(total - middle) * both(removed, lane_low)
        gr_out[:, at] = gr.astype(BF16)
        gk = jnp.exp(last - total) * dot3(v, grad, NN) - jnp.exp(middle - total) * both(
            removed_back, lane_low
        )
        gk_out[:, at] = (gk * ks_ref[:, at] + gka_ref[:, at]).astype(BF16)


def local(receptance, key_input, values, log_decay, kappa_raw, removal, initial_state, out_weight, grad_output):
    size = lax.axis_size("tm")
    frames, width = receptance.shape
    rows_each = PAIRS * HEAD_SIZE // size
    everything = lax.all_gather(grad_output, "tm", axis=0, tiled=True)
    gathered = lax.all_to_all(grad_output, "tm", split_axis=1, concat_axis=0, tiled=True)
    grad_y = lax.dot_general(
        gathered, out_weight, (((0,), (1,)), ((), ())), preferred_element_type=F32
    )
    group = 2
    block = pl.BlockSpec((frames, group * PAIR), lambda i: (0, i))
    per_step = group * size // PAIRS
    pay_shape = (size, HEAD_SIZE + 2 * rows_each, PAIR)
    flat = jax.ShapeDtypeStruct((frames, width), F32)
    params = pltpu.CompilerParams(vmem_limit_bytes=60 << 20)
    payload, *saved = pl.pallas_call(
        functools.partial(first_kernel, rows_each),
        grid=(PAIRS // group,),
        in_specs=[block] * 7,
        out_specs=[pl.BlockSpec((per_step,) + pay_shape[1:], lambda i: (i, 0, 0))] + [block] * SAVED,
        out_shape=[jax.ShapeDtypeStruct(pay_shape, F32)] + [flat] * SAVED,
        compiler_params=params,
        name="first",
    )(receptance, key_input, values, log_decay, kappa_raw, removal, grad_y)
    arrived = lax.all_to_all(payload, "tm", split_axis=0, concat_axis=0, tiled=True)
    start = initial_state.reshape(PAIRS, 2, HEAD_SIZE, HEAD_SIZE).swapaxes(1, 2)
    start = lax.dynamic_slice_in_dim(
        start.reshape(PAIRS * HEAD_SIZE, PAIR), lax.axis_index("tm") * rows_each, rows_each, 0
    )
    entries = pl.pallas_call(
        functools.partial(relay_kernel, rows_each),
        out_shape=jax.ShapeDtypeStruct((size, 2 * rows_each, PAIR), F32),
        compiler_params=params,
        name="relay",
    )(arrived, start)
    entries = lax.all_to_all(entries, "tm", split_axis=0, concat_axis=0, tiled=True)
    state = entries[:, :rows_each].reshape(PAIRS, HEAD_SIZE, PAIR)
    grad = entries[:, rows_each:].reshape(PAIRS, HEAD_SIZE, PAIR)
    small = pl.BlockSpec((group, HEAD_SIZE, PAIR), lambda i: (i, 0, 0))
    low = jax.ShapeDtypeStruct((frames, width), BF16)
    y_low, grad_r, grad_k, grad_v = pl.pallas_call(
        last_kernel,
        grid=(PAIRS // group,),
        in_specs=[small, small] + [block] * (2 + SAVED),
        out_specs=[block] * 4,
        out_shape=[low] * 4,
        compiler_params=params,
        name="last",
    )(state, grad, grad_y, values, *saved)
    y_mine = lax.all_to_all(y_low, "tm", split_axis=1, concat_axis=0, tiled=True)
    loss_scale = 1.0 / math.sqrt(frames * size)
    grad_weight = (
        lax.dot_general(y_mine, everything, (((0,), (1,)), ((), ())), preferred_element_type=F32)
        * loss_scale
    )
    return grad_r, grad_k, grad_v, grad_weight


def solution(mesh):
    rows = P(("groups", "tm"), None)
    return jax.shard_map(
        local,
        mesh=mesh,
        in_specs=(rows,) * 6 + (P("groups", None, None), P(), P("tm", "groups")),
        out_specs=(rows,) * 4,
        check_vma=False,
    )
```

time: 2450 us -> 165 us (0.07); the launches traced: 2410 us -> 165 us
  other arithmetic: 1840 us -> 0 us
  local copies, waits for them, and re-layouts: 238 us -> 8.14 us
  waiting for transfers between devices: 157 us -> 19.3 us
  matrix products: 123 us -> 5.95 us
  Pallas kernels: 0 us -> 58.9 us
  blocking collectives: 0 us -> 52.4 us
    mul x522 -> x0, other arithmetic: 1740 us -> none  [the longest x256 967 us: advance(): projected[..., :, None] * gated_key[..., None, :]]
    mul x176 -> x0, local copies, waits for them, and re-layouts: 155 us -> none  [the longest x24 27.8 us: advance(): value_rows[..., :, None] * keys_in[..., None, :]]
    ppermute x15 -> x0, waiting for transfers between devices: 150 us -> none  [shifted(): return lax.ppermute(x, axis, pairs)]
    dot_general x49 -> x1, matrix products: 121 us -> 4.28 us  [local(): lax.dot_general(y_mine, everything, (((0,), (1,)), ((), ())), preferred_e...]
    while x124 -> x0, other arithmetic: 87.5 us -> none
    pallas_call x0 -> x3, Pallas kernels: none -> 58.9 us  [the longest x1 41.8 us: local(): pl.pallas_call(functools.partial(first_kernel, rows_each), grid=(PAIRS //...]
    all_to_all x0 -> x3, blocking collectives: none -> 52.4 us  [the longest x1 21.1 us: local(): lax.all_to_all(entries, 'tm', split_axis=0, concat_axis=0, tiled=True)]
    while x799 -> x0, local copies, waits for them, and re-layouts: 28.9 us -> none
  transfers between devices with their start and end apart: 19 -> 2, of which waited for: 16 -> 1; matrix products, arithmetic and copies ran while one was open for 41% -> 5% of each run, Pallas kernels for 0% -> 36%
where the time goes in v1:
time: 165 us
  Pallas kernels  58.9 us (36%)
  blocking collectives  52.4 us (32%)
  waiting for transfers between devices  19.3 us (12%)
  between operations  14.1 us (9%)
  local copies, waits for them, and re-layouts  8.14 us (5%)
  matrix products  5.95 us (4%)
  starting transfers between devices  5.93 us (4%)
    pallas_call x1, Pallas kernels, local(): pl.pallas_call(functools.partial(first_kernel, rows_each), grid=(PAIRS //...  41.8 us
    all_to_all x1, blocking collectives, local(): lax.all_to_all(entries, 'tm', split_axis=0, concat_axis=0, tiled=True)  21.1 us
    all_to_all x1, waiting for transfers between devices, local(): lax.all_to_all(payload, 'tm', split_axis=0, concat_axis=0, tiled=True)  18.7 us
    all_to_all x1, blocking collectives, local(): lax.all_to_all(grad_output, 'tm', split_axis=1, concat_axis=0, tiled=True)  17.3 us
    all_to_all x1, blocking collectives, local(): lax.all_to_all(y_low, 'tm', split_axis=1, concat_axis=0, tiled=True)  14 us
    pallas_call x1, Pallas kernels, local(): pl.pallas_call(last_kernel, grid=(PAIRS // group,), in_specs=[small, smal...  11.8 us
    all_to_all x1, starting transfers between devices, local(): lax.all_to_all(payload, 'tm', split_axis=0, concat_axis=0, tiled=True)  5.89 us
    pallas_call x1, Pallas kernels, local(): pl.pallas_call(functools.partial(relay_kernel, rows_each), out_shape=jax....  5.26 us
  transfers between devices with their start and end apart: 2, of which 1 were waited for; matrix products, arithmetic and copies ran while one was open for 5% of the time, Pallas kernels for 36%

profile of v1, /device:TPU:0, one launch (start us, length us, event | category | flops | bytes accessed | tf_op | source)
XLA Modules:
  0.0 164.7 jit_solution(1041735880587036902)
XLA Ops:
  7.2 0.0 copy-start
  7.2 0.0 all-gather.2.cloned.1.call-start
  7.2 0.7 all-gather.2.cloned.1.call-update
  7.9 1.0 copy_bitcast_fusion.1
  8.9 17.3 %all_to_all.48 = bf16[64,16,128]{2,0,1:T(8,128)(2,1)S(1)} all-to-all(bf16[64,16,128]{2,0,1:T(8,128)(2,1)S(1)} %copy_bitcast_fusion.1), channel_id=1, replica_groups=mesh['groups'=2,'tm'=16] {'tm'}, dimensions={1} | all-to-all | bytes 524288 | tf_op jit(solution)/shard_map/all_to_all | solution.py:249
  26.3 0.0 copy-done
  26.3 1.7 %fusion.3.gy_ref = f32[128,1024]{1,0:T(8,128)} fusion(bf16[1024,128]{1,0:T(8,128)(2,1)S(1)} %bitcast.30, bf16[1024,1024]{1,0:T(8,128)(2,1)S(1)} %copy-done), kind=kOutput, calls=%fused_computation.7 | convolution fusion | flops 268435456 | bytes 2883584 | tf_op jit(solution)/shard_map/dot_general | solution.py:250
  27.9 41.8 %first.1 = (f32[16,128,128]{2,1,0:T(8,128)}, f32[128,1024]{1,0:T(8,128)}, f32[128,1024]{1,0:T(8,128)}, f32[128,1024]{1,0:T(8,128)}, f32[128,1024]{1,0:T(8,128)},...) custom-call(bf16[128,1024]{1,0:T(8,128)(2,1)} %rec_ref.1, ...), custom_call_target="tpu_custom_call" | custom-call | tf_op jit(solution)/shard_map/first/pallas_call | solution.py:259
  69.8 5.9 %all-to-all-start.1 = ((f32[16,128,128]{2,1,0:T(8,128)}), f32[16,128,128]{2,1,0:T(8,128)S(1)}, u32[]{:S(2)}, u32[]{:S(2)}) async-start(f32[16,128,128]{2,1,0:T(8,128)} %get-tuple-element.23), calls=%async_computation.1 | async-start | bytes 2097152 | tf_op jit(solution)/shard_map/all_to_all | solution.py:268
  75.7 2.3 %copy.33 = f32[8,2,64,64]{3,1,2,0:T(2,128)} copy(f32[8,2,64,64]{3,2,1,0:T(8,128)} %bitcast.31) | data formatting | bytes 524288 | tf_op jit(solution)/shard_map/reshape | solution.py:269
  77.9 1.3 reshape.27
  79.3 0.6 constant_dynamic-slice_fusion.start_ref
  79.9 18.7 %all-to-all-done.1.pay_ref = f32[16,128,128]{2,1,0:T(8,128)S(1)} async-done(((f32[16,128,128]{2,1,0:T(8,128)}), f32[16,128,128]{2,1,0:T(8,128)S(1)}, u32[]{:S(2)}, u32[]{:S(2)}) %all-to-all-start.1) | async-done | bytes 1048608 | tf_op jit(solution)/shard_map/all_to_all | solution.py:268
  98.6 0.0 copy-start.1
  98.6 1.0 copy-done.1
  99.5 5.3 %relay.1 = f32[16,64,128]{2,1,0:T(8,128)} custom-call(f32[16,128,128]{2,1,0:T(8,128)} %copy-done.1, f32[32,128]{1,0:T(8,128)} %constant_dynamic-slice_fusion.start_ref), custom_call_target="tpu_custom_call" | custom-call | tf_op jit(solution)/shard_map/relay/pallas_call | solution.py:273
  104.8 21.1 %all_to_all.49 = f32[16,64,128]{2,1,0:T(8,128)S(1)} all-to-all(f32[16,64,128]{2,1,0:T(8,128)} %relay.1), channel_id=1, replica_groups=mesh['groups'=2,'tm'=16] {'tm'}, dimensions={0} | all-to-all | bytes 1048576 | tf_op jit(solution)/shard_map/all_to_all | solution.py:279
  125.8 0.8 fusion.2
  126.7 11.8 %last.1 = (bf16[128,1024]{1,0:T(8,128)(2,1)}, bf16[128,1024]{1,0:T(8,128)(2,1)}, bf16[128,1024]{1,0:T(8,128)(2,1)}, bf16[128,1024]{1,0:T(8,128)(2,1)}) custom-call(f32[8,64,128]{2,1,0:T(8,128)} %bitcast.28, f32[8,64,128]{2,1,0:T(8,128)} %bitcast.27, f32[128,1024]{1,0:T(8,128)} %fusion.3.gy_ref, bf16[128,1024]{1,0:T(8,128)(2,1)} %val_ref.3, ...), custom_call_target="tpu_custom_call" | custom-call | tf_op jit(solution)/shard_map/last/pallas_call | solution.py:284
  138.5 1.1 copy.23
  139.6 14.0 %all_to_all.50 = bf16[128,16,64]{0,2,1:T(8,128)(2,1)S(1)} all-to-all(bf16[128,16,64]{0,2,1:T(8,128)(2,1)S(1)} %bitcast.29), channel_id=1, replica_groups=mesh['groups'=2,'tm'=16] {'tm'}, dimensions={1} | all-to-all | bytes 524288 | tf_op jit(solution)/shard_map/all_to_all | solution.py:293
  153.6 0.0 all-gather.2.cloned.1.call-done
  153.6 4.3 %convolution_multiply_fusion = f32[64,1024]{1,0:T(8,128)} fusion(bf16[1024,2048]{1,0:T(8,128)(2,1)} %all-gather.2.cloned.1.call-done, bf16[128,16,64]{0,2,1:T(8,128)(2,1)S(1)} %all_to_all.50), kind=kOutput, calls=%fused_computation | convolution fusion | flops 268500992 | bytes 4718592 | tf_op jit(solution)/shard_map/dot_general | solution.py:296
Async XLA Ops:
  7.2 19.1 %copy-start = (bf16[1024,1024]{1,0:T(8,128)(2,1)S(1)}, bf16[1024,1024]{1,0:T(8,128)(2,1)}, u32[]{:S(2)}) copy-start(bf16[1024,1024]{1,0:T(8,128)(2,1)} %param.16) | copy-start | bytes 6291460
  7.2 146.4 %all-gather.2.cloned.1.call-start = ((), (), s32[]{:S(2)}) async-start(), calls=%async_computation.4 | async-start | bytes 4456448 | tf_op jit(solution)/shard_map/all_gather | solution.py:248
  69.8 28.8 %all-to-all-start.1 = ((f32[16,128,128]{2,1,0:T(8,128)}), f32[16,128,128]{2,1,0:T(8,128)S(1)}, u32[]{:S(2)}, u32[]{:S(2)}) async-start(f32[16,128,128]{2,1,0:T(8,128)} %get-tuple-element.23), calls=%async_computation.1 | async-start | bytes 2097152 | tf_op jit(solution)/shard_map/all_to_all | solution.py:268
  98.6 1.0 copy-start.1
Sparse Core Ops, SparseCore 0:
  10.1 53.9 all-gather.1

commit v2 on v1

v2 whole, which is shorter than its diff:
```python
import functools
import math

import jax
import jax.numpy as jnp
from jax import lax
from jax.experimental import pallas as pl
from jax.experimental.pallas import tpu as pltpu
from jax.sharding import PartitionSpec as P

HEAD_COUNT = 16
HEAD_SIZE = 64
PAIR = 2 * HEAD_SIZE
PAIRS = HEAD_COUNT // 2
F32 = jnp.float32
BF16 = jnp.bfloat16

NN = (((1,), (0,)), ((), ()))
NT = (((1,), (1,)), ((), ()))
TN = (((0,), (0,)), ((), ()))


def split(x):
    high = x.astype(BF16)
    return high, (x - high.astype(F32)).astype(BF16)


def dot1(a, b, dims):
    return lax.dot_general(a, b, dims, preferred_element_type=F32)


def dot3(a, b, dims):
    a = (a,) if not isinstance(a, tuple) and a.dtype == BF16 else a if isinstance(a, tuple) else split(a)
    b = (b,) if not isinstance(b, tuple) and b.dtype == BF16 else b if isinstance(b, tuple) else split(b)
    out = dot1(a[0], b[0], dims)
    if len(b) > 1:
        out = out + dot1(a[0], b[1], dims)
    if len(a) > 1:
        out = out + dot1(a[1], b[0], dims)
    return out


def iota(shape, dim):
    return lax.broadcasted_iota(jnp.int32, shape, dim)


def both(f, lane_low):
    return jnp.where(lane_low, f(0), f(1))


def pack(full, lane_low):
    return jnp.where(lane_low, full[:HEAD_SIZE], full[HEAD_SIZE:])


def unpack(packed, diagonal):
    return jnp.where(diagonal, jnp.concatenate([packed, packed], 0), 0.0)


def inverses(lower, row, col):
    size = row.shape[0]
    eye = jnp.where(row == col, 1.0, 0.0).astype(F32)
    step = 1
    out = None
    while step < size:
        inside = (row // (2 * step) == col // (2 * step)) & (row // step != col // step)
        off = [jnp.where(inside, m, 0.0) for m in lower]
        if out is None:
            out = [eye - m for m in off]
        else:
            halves = [split(t) for t in out]
            mid = [dot3(m, t, NN) for m, t in zip(off, halves)]
            out = [t - dot3(h, m, NN) for t, h, m in zip(out, halves, mid)]
        step *= 2
    return out


GROUP = 2


def one_less_exp(x):
    series = jnp.full_like(x, 1.0 / math.factorial(10))
    for n in range(9, 0, -1):
        series = series * x + 1.0 / math.factorial(n)
    return jnp.where(x > -0.5, -x * series, 1.0 - jnp.exp(x))


def row_scales(total):
    frames = total.shape[0]
    return total[frames // 2 - 1 : frames // 2], total[frames - 1 : frames]


def forward_kernel(rows_each, rec_ref, key_ref, val_ref, log_ref, kap_ref, rem_ref, pay_ref,
                   u_ref, x_ref, y_ref, yr_ref, tot_ref, ks_ref, a_ref, b_ref, k_ref,
                   t_ref, ak_ref, rb_ref, rk_ref):
    frames = rec_ref.shape[0]
    row, col = iota((frames, frames), 0), iota((frames, frames), 1)
    lane_low = iota((frames, PAIR), 1) < HEAD_SIZE
    low2 = jnp.concatenate([lane_low, lane_low], 1)
    pack_low = iota((HEAD_SIZE, PAIR), 1) < HEAD_SIZE
    prow, pcol = iota((PAIR, PAIR), 0), iota((PAIR, PAIR), 1)
    ones = jnp.where((prow // HEAD_SIZE) == (pcol // HEAD_SIZE), 1.0, 0.0).astype(BF16)
    tri = jnp.where(row >= col, 1.0, 0.0).astype(BF16)
    own2 = [jnp.concatenate([m, m], 0) for m in (lane_low, jnp.logical_not(lane_low))]
    strict, lax_tri = row > col, row >= col
    zero = jnp.zeros((), BF16)
    count = rec_ref.shape[1] // PAIR

    m_ab = []
    for pair in range(count):
        at = pl.ds(pair * PAIR, PAIR)
        log_low = log_ref[:, at]
        log_part = log_low.astype(F32)
        total = dot1(tri, log_low, NN)
        middle, last = row_scales(total)
        key_scale = jnp.sqrt(one_less_exp(log_part))
        raw = kap_ref[:, at].astype(F32)
        norm = dot3(raw * raw, ones, NN)
        a = raw / jnp.sqrt(norm + 1e-06)
        e_neg = jnp.exp(middle - total)
        a_mid = a * jnp.exp(total - log_part - middle)
        b_mid = rem_ref[:, at].astype(F32) * a * e_neg
        k_mid = key_ref[:, at].astype(F32) * key_scale * e_neg
        r_mid = rec_ref[:, at].astype(F32) * jnp.exp(total - middle)
        for ref, value in zip((tot_ref, ks_ref, a_ref, b_ref, k_ref), (total, key_scale, a_mid, b_mid, k_mid)):
            ref[:, at] = value
        upper = split(jnp.concatenate([a_mid, r_mid], 0))
        rights = split(jnp.concatenate([b_mid, k_mid], 0))
        for h, m in enumerate(own2):
            gram = dot3(upper, tuple(jnp.where(m, x, zero) for x in rights), NT)
            head = pl.ds((pair * 2 + h) * frames, frames)
            m_ab.append(jnp.where(strict, gram[:frames, :frames], 0.0))
            ak_ref[:, head] = jnp.where(strict, gram[:frames, frames:], 0.0)
            rb_ref[:, head] = jnp.where(lax_tri, gram[frames:, :frames], 0.0)
            rk_ref[:, head] = jnp.where(lax_tri, gram[frames:, frames:], 0.0)
    inverted = inverses(m_ab, row, col)

    for pair in range(count):
        at = pl.ds(pair * PAIR, PAIR)
        heads = [pl.ds((pair * 2 + h) * frames, frames) for h in range(2)]
        v = val_ref[:, at]
        total = tot_ref[:, at]
        middle, last = row_scales(total)
        a_abs = a_ref[:, at] * jnp.exp(middle)
        r_abs = rec_ref[:, at].astype(F32) * jnp.exp(total)
        scale = jnp.exp(last - middle)
        for h in range(2):
            t_ref[:, heads[h]] = inverted[pair * 2 + h]
        t_inv = [split(inverted[pair * 2 + h]) for h in range(2)]
        on_v = [dot3(jnp.concatenate([ak_ref[:, h], rk_ref[:, h]], 0), v, NN) for h in heads]
        on_v = jnp.where(own2[0], on_v[0], on_v[1])
        given = split(jnp.concatenate([on_v[:frames], a_abs], 1))
        inner = both(lambda h: dot3(t_inv[h], given, NN), low2)
        u_ref[:, at], x_ref[:, at] = inner[:, :PAIR], inner[:, PAIR:]
        inner = split(inner)
        minus = both(lambda h: dot3(rb_ref[:, heads[h]], inner, NN), low2)
        y_ref[:, at] = on_v[frames:] - minus[:, :PAIR]
        yr_ref[:, at] = r_abs - minus[:, PAIR:]
        ended = dot3(inner, b_ref[:, at] * scale, TN)
        through = pack(jnp.where(prow == pcol, jnp.exp(last), 0.0) - ended[PAIR:], pack_low)
        offset = pack(dot3(v, k_ref[:, at] * scale, TN) - ended[:PAIR], pack_low)
        for part in range(HEAD_SIZE // rows_each):
            to = pair * (HEAD_SIZE // rows_each) + part
            pay_ref[to, :HEAD_SIZE] = through
            pay_ref[to, HEAD_SIZE:] = offset[part * rows_each : (part + 1) * rows_each]


def backward_kernel(rows_each, rec_ref, val_ref, gy_ref, tot_ref, ks_ref, a_ref, b_ref, k_ref,
                    t_ref, ak_ref, rb_ref, rk_ref,
                    pay_ref, p_ref, tb_ref, gv_ref, gvk_ref, gra_ref, gka_ref):
    frames = rec_ref.shape[0]
    row, col = iota((frames, frames), 0), iota((frames, frames), 1)
    lane_low = iota((frames, PAIR), 1) < HEAD_SIZE
    own = [lane_low, jnp.logical_not(lane_low)]
    low2 = jnp.concatenate([lane_low, lane_low], 1)
    pack_low = iota((HEAD_SIZE, PAIR), 1) < HEAD_SIZE
    zero = jnp.zeros((), BF16)
    for pair in range(rec_ref.shape[1] // PAIR):
        at = pl.ds(pair * PAIR, PAIR)
        heads = [pl.ds((pair * 2 + h) * frames, frames) for h in range(2)]
        total = tot_ref[:, at]
        middle, last = row_scales(total)
        scale = jnp.exp(last - middle)
        v, q = val_ref[:, at], split(gy_ref[:, at])
        e_pos, e_neg = jnp.exp(total - middle), jnp.exp(middle - total)
        r = rec_ref[:, at].astype(F32)
        m_rb, m_rk, m_ak, t_inv = (
            [split(ref[:, h]) for h in heads] for ref in (rb_ref, rk_ref, ak_ref, t_ref)
        )
        back = both(lambda h: dot3(m_rb[h], q, TN), lane_low)
        given = split(jnp.concatenate([back, b_ref[:, at] * scale], 1))
        pulled = both(lambda h: dot3(t_inv[h], given, TN), low2)
        p0 = pulled[:, :PAIR]
        p_ref[:, at], tb_ref[:, at] = p0, pulled[:, PAIR:]
        pulled = split(pulled)
        minus = both(lambda h: dot3(m_ak[h], pulled, TN), low2)
        gv_ref[:, at] = both(lambda h: dot3(m_rk[h], q, TN), lane_low) - minus[:, :PAIR]
        gvk_ref[:, at] = k_ref[:, at] * scale - minus[:, PAIR:]
        v_own = [jnp.where(m, v, zero) for m in own]
        q_own = [tuple(jnp.where(m, x, zero) for x in q) for m in own]
        k_mid, r_mid = split(k_ref[:, at]), split(r * e_pos)
        gra_ref[:, at] = e_pos * both(
            lambda h: dot3(jnp.where(row >= col, dot3(q, v_own[h], NT), 0.0), k_mid, NN), lane_low
        )
        gka_ref[:, at] = ks_ref[:, at] * e_neg * both(
            lambda h: dot3(jnp.where(row <= col, dot3(v, q_own[h], NT), 0.0), r_mid, NN), lane_low
        )
        pull = dot3(q, r * jnp.exp(total), TN) - dot3(p0, a_ref[:, at] * jnp.exp(middle), TN)
        pull = pack(pull, pack_low)
        for part in range(HEAD_SIZE // rows_each):
            to = pair * (HEAD_SIZE // rows_each) + part
            pay_ref[to] = pull[part * rows_each : (part + 1) * rows_each]


def relay_kernel(rows_each, pay_ref, pull_ref, start_ref, out_ref):
    count = pay_ref.shape[0]
    diagonal = (iota((PAIR, PAIR), 0) // HEAD_SIZE) == (iota((PAIR, PAIR), 1) // HEAD_SIZE)

    def lap(i, carried):
        state, grad = carried
        j = count - 1 - i
        out_ref[i, :rows_each] = state
        out_ref[j, rows_each:] = grad
        state = pay_ref[i, HEAD_SIZE:] + dot3(
            state, unpack(pay_ref[i, :HEAD_SIZE], diagonal), NN
        )
        grad = pull_ref[j] + dot3(
            grad, unpack(pay_ref[j, :HEAD_SIZE], diagonal), NT
        )
        return state, grad

    lax.fori_loop(0, count, lap, (start_ref[...], jnp.zeros((rows_each, PAIR), F32)))


def output_kernel(state_ref, y_ref, yr_ref, ylow_ref):
    diagonal = (iota((PAIR, PAIR), 0) // HEAD_SIZE) == (iota((PAIR, PAIR), 1) // HEAD_SIZE)
    for pair in range(y_ref.shape[1] // PAIR):
        at = pl.ds(pair * PAIR, PAIR)
        state = unpack(state_ref[pair], diagonal)
        y = y_ref[:, at] + dot3(yr_ref[:, at], state, NT)
        ylow_ref[pl.ds(pair * PAIR, PAIR), :] = y.T.astype(BF16)


def last_kernel(state_ref, grad_ref, gy_ref, val_ref, u_ref, x_ref, p_ref, tb_ref,
                gv_ref, gvk_ref, gra_ref, gka_ref, tot_ref, b_ref, a_ref, ks_ref,
                gr_out, gk_out, gv_out):
    frames = gy_ref.shape[0]
    row, col = iota((frames, frames), 0), iota((frames, frames), 1)
    lane_low = iota((frames, PAIR), 1) < HEAD_SIZE
    own = [lane_low, jnp.logical_not(lane_low)]
    diagonal = (iota((PAIR, PAIR), 0) // HEAD_SIZE) == (iota((PAIR, PAIR), 1) // HEAD_SIZE)
    zero = jnp.zeros((), BF16)
    for pair in range(gy_ref.shape[1] // PAIR):
        at = pl.ds(pair * PAIR, PAIR)
        state = split(unpack(state_ref[pair], diagonal))
        grad = split(unpack(grad_ref[pair], diagonal))
        q, v = split(gy_ref[:, at]), val_ref[:, at]
        u = split(u_ref[:, at] + dot3(x_ref[:, at], state, NT))
        behind = dot3(jnp.concatenate([tb_ref[:, at], gvk_ref[:, at]], 0), grad, NT)
        p = split(p_ref[:, at] + behind[:frames])
        gv_out[:, at] = (gv_ref[:, at] + behind[frames:]).astype(BF16)
        b_mid, a_mid = split(b_ref[:, at]), split(a_ref[:, at])
        total = tot_ref[:, at]
        middle, last = total[frames // 2 - 1 : frames // 2], total[frames - 1 : frames]

        def removed(h):
            gram = dot3(q, tuple(jnp.where(own[h], x, zero) for x in u), NT)
            return dot3(jnp.where(row >= col, gram, 0.0), b_mid, NN)

        def removed_back(h):
            gram = dot3(v, tuple(jnp.where(own[h], x, zero) for x in p), NT)
            return dot3(jnp.where(row < col, gram, 0.0), a_mid, NN)

        gr = jnp.exp(total) * dot3(q, state, NN) + gra_ref[:, at]
        gr = gr - jnp.exp(total - middle) * both(removed, lane_low)
        gr_out[:, at] = gr.astype(BF16)
        gk = jnp.exp(last - total) * dot3(v, grad, NN) - jnp.exp(middle - total) * both(
            removed_back, lane_low
        )
        gk_out[:, at] = (gk * ks_ref[:, at] + gka_ref[:, at]).astype(BF16)


def cost(flops, moved):
    return pl.CostEstimate(flops=flops, bytes_accessed=moved, transcendentals=0)


def local(receptance, key_input, values, log_decay, kappa_raw, removal, initial_state, out_weight, grad_output):
    size = lax.axis_size("tm")
    frames, width = receptance.shape
    rows_each = PAIRS * HEAD_SIZE // size
    everything = lax.all_gather(grad_output, "tm", axis=0, tiled=True)
    gathered = lax.all_to_all(grad_output, "tm", split_axis=1, concat_axis=0, tiled=True)
    group = GROUP
    block = pl.BlockSpec((frames, group * PAIR), lambda i: (0, i))
    square = pl.BlockSpec((frames, group * 2 * frames), lambda i: (0, i))
    per_step = group * size // PAIRS
    flat = jax.ShapeDtypeStruct((frames, width), F32)
    matrix = jax.ShapeDtypeStruct((frames, HEAD_COUNT * frames), F32)
    low = jax.ShapeDtypeStruct((frames, width), BF16)
    params = pltpu.CompilerParams(vmem_limit_bytes=60 << 20)
    steps = (PAIRS // group,)

    def sent(rows):
        return (
            pl.BlockSpec((per_step, rows, PAIR), lambda i: (i, 0, 0)),
            jax.ShapeDtypeStruct((size, rows, PAIR), F32),
        )

    spec, shape = sent(HEAD_SIZE + rows_each)
    payload, u0, x0, y0, yr, total, scale, a, b, k, t, ak, rb, rk = pl.pallas_call(
        functools.partial(forward_kernel, rows_each),
        grid=steps,
        in_specs=[block] * 6,
        out_specs=[spec] + [block] * 9 + [square] * 4,
        out_shape=[shape] + [flat] * 9 + [matrix] * 4,
        compiler_params=params,
        cost_estimate=cost(20 << 30, 10 << 20),
        name="forward",
    )(receptance, key_input, values, log_decay, kappa_raw, removal)
    arrived = lax.all_to_all(payload, "tm", split_axis=0, concat_axis=0, tiled=True)
    grad_y = lax.dot_general(
        gathered, out_weight, (((0,), (1,)), ((), ())), preferred_element_type=F32
    )
    spec, shape = sent(rows_each)
    pull, p0, tb, gv, gvk, gra, gka = pl.pallas_call(
        functools.partial(backward_kernel, rows_each),
        grid=steps,
        in_specs=[block] * 8 + [square] * 4,
        out_specs=[spec] + [block] * 6,
        out_shape=[shape] + [flat] * 6,
        compiler_params=params,
        cost_estimate=cost(12 << 30, 10 << 20),
        name="backward",
    )(receptance, values, grad_y, total, scale, a, b, k, t, ak, rb, rk)
    arrived, pull = lax.optimization_barrier((arrived, pull))
    pull = lax.all_to_all(pull, "tm", split_axis=0, concat_axis=0, tiled=True)
    start = initial_state.reshape(PAIRS, 2, HEAD_SIZE, HEAD_SIZE).swapaxes(1, 2)
    start = lax.dynamic_slice_in_dim(
        start.reshape(PAIRS * HEAD_SIZE, PAIR), lax.axis_index("tm") * rows_each, rows_each, 0
    )
    entries = pl.pallas_call(
        functools.partial(relay_kernel, rows_each),
        out_shape=jax.ShapeDtypeStruct((size, 2 * rows_each, PAIR), F32),
        compiler_params=params,
        name="relay",
    )(arrived, pull, start)
    entries = lax.all_to_all(entries, "tm", split_axis=0, concat_axis=0, tiled=True)
    state = entries[:, :rows_each].reshape(PAIRS, HEAD_SIZE, PAIR)
    grad = entries[:, rows_each:].reshape(PAIRS, HEAD_SIZE, PAIR)
    small = pl.BlockSpec((group, HEAD_SIZE, PAIR), lambda i: (i, 0, 0))
    y_low = pl.pallas_call(
        output_kernel,
        grid=steps,
        in_specs=[small, block, block],
        out_specs=pl.BlockSpec((group * PAIR, frames), lambda i: (i, 0)),
        out_shape=jax.ShapeDtypeStruct((width, frames), BF16),
        compiler_params=params,
        cost_estimate=cost(1 << 28, 2 << 20),
        name="output",
    )(state, y0, yr)
    y_low = y_low.reshape(size, width // size, frames)
    y_mine = lax.all_to_all(y_low, "tm", split_axis=0, concat_axis=0, tiled=True)
    grad_r, grad_k, grad_v = pl.pallas_call(
        last_kernel,
        grid=steps,
        in_specs=[small, small] + [block] * 14,
        out_specs=[block] * 3,
        out_shape=[low] * 3,
        compiler_params=params,
        cost_estimate=cost(8 << 30, 8 << 20),
        name="last",
    )(state, grad, grad_y, values, u0, x0, p0, tb, gv, gvk, gra, gka, total, b, a, scale)
    loss_scale = 1.0 / math.sqrt(frames * size)
    y_mine = y_mine.swapaxes(0, 1).reshape(width // size, size * frames)
    grad_weight = (
        lax.dot_general(y_mine, everything, (((1,), (1,)), ((), ())), preferred_element_type=F32)
        * loss_scale
    )
    return grad_r, grad_k, grad_v, grad_weight


def solution(mesh):
    rows = P(("groups", "tm"), None)
    return jax.shard_map(
        local,
        mesh=mesh,
        in_specs=(rows,) * 6 + (P("groups", None, None), P(), P("tm", "groups")),
        out_specs=(rows,) * 4,
        check_vma=False,
    )
```

time: 165 us -> 149 us (0.903)
  blocking collectives: 52.4 us -> 17.8 us
  starting transfers between devices: 5.93 us -> 24.5 us
  waiting for transfers between devices: 19.3 us -> 21.1 us
  local copies, waits for them, and re-layouts: 8.14 us -> 6.35 us
    all_to_all x2 -> x0, blocking collectives: 31.3 us -> none  [the longest x1 17.3 us: local(): lax.all_to_all(grad_output, 'tm', split_axis=1, concat_axis=0, tiled=True)]
    all_to_all x0 -> x3, starting transfers between devices: none -> 18.5 us  [the longest x1 7.41 us: local(): lax.all_to_all(grad_output, 'tm', split_axis=1, concat_axis=0, tiled=True)]
    all_to_all x0 -> x3, waiting for transfers between devices: none -> 6.27 us  [the longest x1 6.27 us: local(): pull = lax.all_to_all(pull, 'tm', split_axis=0, concat_axis=0, tiled=True)]
    all_to_all x1, waiting for transfers between devices: 18.7 us -> 14.2 us  [local(): lax.all_to_all(payload, 'tm', split_axis=0, concat_axis=0, tiled=True)]
    all_to_all x1, blocking collectives: 21.1 us -> 17.8 us  [local(): lax.all_to_all(entries, 'tm', split_axis=0, concat_axis=0, tiled=True)]
    pallas_call x2 -> x4, Pallas kernels: 53.7 us -> 53.1 us  [the longest x1 20.4 us: local(): pl.pallas_call(functools.partial(forward_kernel, rows_each), grid=steps,...]
  transfers between devices with their start and end apart: 2 -> 5, of which waited for: 1 -> 2; matrix products, arithmetic and copies ran while one was open for 5% -> 5% of each run, Pallas kernels for 36% -> 39%
where the time goes in v2:
time: 149 us; the launch traced here: 148 us
  Pallas kernels  58.3 us (39%)
  starting transfers between devices  24.5 us (16%)
  waiting for transfers between devices  21.1 us (14%)
  blocking collectives  17.8 us (12%)
  between operations  14.1 us (9%)
  local copies, waits for them, and re-layouts  6.35 us (4%)
  matrix products  5.9 us (4%)
    pallas_call x1, Pallas kernels, local(): pl.pallas_call(functools.partial(forward_kernel, rows_each), grid=steps,...  20.4 us
    all_to_all x1, blocking collectives, local(): lax.all_to_all(entries, 'tm', split_axis=0, concat_axis=0, tiled=True)  17.8 us
    pallas_call x1, Pallas kernels, local(): pl.pallas_call(functools.partial(backward_kernel, rows_each), grid=steps,...  15.7 us
    all_to_all x1, waiting for transfers between devices, local(): lax.all_to_all(payload, 'tm', split_axis=0, concat_axis=0, tiled=True)  14.2 us
    pallas_call x1, Pallas kernels, local(): pl.pallas_call(last_kernel, grid=steps, in_specs=[small, small] + [block]...  13 us
    all_to_all x1, starting transfers between devices, local(): lax.all_to_all(grad_output, 'tm', split_axis=1, concat_axis=0, tiled=True)  7.41 us
    all_to_all x1, starting transfers between devices, local(): pull = lax.all_to_all(pull, 'tm', split_axis=0, concat_axis=0, tiled=True)  6.95 us
    all_to_all x1, waiting for transfers between devices, local(): pull = lax.all_to_all(pull, 'tm', split_axis=0, concat_axis=0, tiled=True)  6.27 us
  transfers between devices with their start and end apart: 5, of which 2 were waited for; matrix products, arithmetic and copies ran while one was open for 5% of the time, Pallas kernels for 39%

profile of v2, /device:TPU:0, one launch (start us, length us, event | category | flops | bytes accessed | tf_op | source)
XLA Modules:
  0.0 148.1 jit_solution(11006060302336648946)
XLA Ops:
  7.2 0.0 copy-start
  7.2 0.0 all-gather.2.cloned.1.call-start
  7.2 0.7 all-gather.2.cloned.1.call-update
  7.9 1.7 %copy_bitcast_fusion.1 = bf16[64,16,128]{2,0,1:T(8,128)(2,1)} fusion(bf16[64,2048]{1,0:T(8,128)(2,1)} %param.17), kind=kLoop, calls=%fused_computation.4 | loop fusion | bytes 524288 | tf_op jit(solution)/shard_map/all_to_all | solution.py:291
  9.6 7.4 %all-to-all-start.1 = ((bf16[64,16,128]{2,0,1:T(8,128)(2,1)}), bf16[64,16,128]{2,0,1:T(8,128)(2,1)S(1)}, u32[]{:S(2)}, u32[]{:S(2)}) async-start(bf16[64,16,128]{2,0,1:T(8,128)(2,1)} %copy_bitcast_fusion.1), calls=%async_computation.1 | async-start | bytes 524288 | tf_op jit(solution)/shard_map/all_to_all | solution.py:291
  17.1 20.4 %forward.1 = (f32[16,96,128]{2,1,0:T(8,128)}, f32[128,1024]{1,0:T(8,128)}, f32[128,1024]{1,0:T(8,128)}, f32[128,1024]{1,0:T(8,128)}, f32[128,1024]{1,0:T(8,128)}...) custom-call(bf16[128,1024]{1,0:T(8,128)(2,1)} %rec_ref.3, ...), custom_call_target="tpu_custom_call" | custom-call | flops 21474836480 | bytes 10485760 | tf_op jit(solution)/shard_map/forward/pallas_call | solution.py:309
  37.4 0.0 all-to-all-done.1
  37.4 6.0 %all-to-all-start = ((f32[16,96,128]{2,1,0:T(8,128)}), f32[16,96,128]{2,1,0:T(8,128)S(1)}, u32[]{:S(2)}, u32[]{:S(2)}) async-start(f32[16,96,128]{2,1,0:T(8,128)} %get-tuple-element.30), calls=%async_computation | async-start | bytes 1572864 | tf_op jit(solution)/shard_map/all_to_all | solution.py:319
  43.4 0.0 copy-done
  43.5 1.6 %fusion.3.gy_ref = f32[128,1024]{1,0:T(8,128)} fusion(bf16[1024,128]{1,0:T(8,128)(2,1)S(1)} %bitcast.30, bf16[1024,1024]{1,0:T(8,128)(2,1)S(1)} %copy-done), kind=kOutput, calls=%fused_computation.7 | convolution fusion | flops 268435456 | bytes 2883584 | tf_op jit(solution)/shard_map/dot_general | solution.py:320
  45.1 15.7 %backward.1 = (f32[16,32,128]{2,1,0:T(8,128)}, f32[128,1024]{1,0:T(8,128)}, f32[128,1024]{1,0:T(8,128)}, f32[128,1024]{1,0:T(8,128)}, f32[128,1024]{1,0:T(8,128)...) custom-call(bf16[128,1024]{1,0:T(8,128)(2,1)} %rec_ref.3, bf16[128,1024]{1,0:T(8,128)(2,1)} %val_ref.5, ...), custom_call_target="tpu_custom_call" | custom-call | flops 12884901888 | bytes 10485760 | tf_op jit(solution)/shard_map/backward/pallas_call | solution.py:324
  60.8 14.2 %all-to-all-done.pay_ref = f32[16,96,128]{2,1,0:T(8,128)S(1)} async-done(((f32[16,96,128]{2,1,0:T(8,128)}), f32[16,96,128]{2,1,0:T(8,128)S(1)}, u32[]{:S(2)}, u32[]{:S(2)}) %all-to-all-start) | async-done | bytes 786464 | tf_op jit(solution)/shard_map/all_to_all | solution.py:319
  74.9 0.0 copy-start.1
  74.9 7.0 %all-to-all-start.2 = ((f32[16,32,128]{2,1,0:T(8,128)}), f32[16,32,128]{2,1,0:T(8,128)}, u32[]{:S(2)}, u32[]{:S(2)}) async-start(f32[16,32,128]{2,1,0:T(8,128)} %get-tuple-element.42), calls=%async_computation.2 | async-start | bytes 524288 | tf_op jit(solution)/shard_map/all_to_all | solution.py:335
  81.9 1.5 copy.30
  83.4 1.0 reshape.30
  84.4 1.3 constant_dynamic-slice_fusion.start_ref
  85.7 6.3 %all-to-all-done.2.pull_ref = f32[16,32,128]{2,1,0:T(8,128)} async-done(((f32[16,32,128]{2,1,0:T(8,128)}), f32[16,32,128]{2,1,0:T(8,128)}, u32[]{:S(2)}, u32[]{:S(2)}) %all-to-all-start.2) | async-done | bytes 262176 | tf_op jit(solution)/shard_map/all_to_all | solution.py:335
  92.0 0.0 copy-done.1
  92.0 5.2 %relay.1 = f32[16,64,128]{2,1,0:T(8,128)} custom-call(f32[16,96,128]{2,1,0:T(8,128)} %copy-done.1, f32[16,32,128]{2,1,0:T(8,128)} %all-to-all-done.2.pull_ref, f32[32,128]{1,0:T(8,128)} %constant_dynamic-slice_fusion.start_ref), custom_call_target="tpu_custom_call" | custom-call | tf_op jit(solution)/shard_map/relay/pallas_call | solution.py:340
  97.2 17.8 %all_to_all.39 = f32[16,64,128]{2,1,0:T(8,128)S(1)} all-to-all(f32[16,64,128]{2,1,0:T(8,128)} %relay.1), channel_id=1, replica_groups=mesh['groups'=2,'tm'=16] {'tm'}, dimensions={0} | all-to-all | bytes 1048576 | tf_op jit(solution)/shard_map/all_to_all | solution.py:346
  115.0 0.8 fusion.2
  115.8 4.0 %output.1 = bf16[1024,128]{1,0:T(8,128)(2,1)} custom-call(f32[8,64,128]{2,1,0:T(8,128)} %bitcast.28, f32[128,1024]{1,0:T(8,128)} %get-tuple-element.54.y_ref, f32[128,1024]{1,0:T(8,128)} %get-tuple-element.55.yr_ref), custom_call_target="tpu_custom_call" | custom-call | flops 268435456 | bytes 2097152 | tf_op jit(solution)/shard_map/output/pallas_call | solution.py:350
  119.8 4.1 %all-to-all-start.4 = ((bf16[16,64,128]{2,1,0:T(8,128)(2,1)}), bf16[16,64,128]{2,1,0:T(8,128)(2,1)S(1)}, u32[]{:S(2)}, u32[]{:S(2)}) async-start(bf16[16,64,128]{2,1,0:T(8,128)(2,1)} %bitcast.27), calls=%async_computation.4 | async-start | bytes 524288 | tf_op jit(solution)/shard_map/all_to_all | solution.py:361
  123.9 13.0 %last.1 = (bf16[128,1024]{1,0:T(8,128)(2,1)}, bf16[128,1024]{1,0:T(8,128)(2,1)}, bf16[128,1024]{1,0:T(8,128)(2,1)}) custom-call(f32[8,64,128]{2,1,0:T(8,128)} %bitcast.29, f32[8,64,128]{2,1,0:T(8,128)} %bitcast.32, f32[128,1024]{1,0:T(8,128)} %fusion.3.gy_ref, bf16[128,1024]{1,0:T(8,128)(2,1)} %val_ref.5, f32[128,1024]{1,0:T(8,128)} %get-tuple-element.43.u_ref, ...), custom_call_target="tpu_custom_call" | custom-call | flops 8589934592 | bytes 8388608 | tf_op jit(solution)/shard_map/last/pallas_call | solution.py:362
  136.9 0.0 all-to-all-done.4
  137.0 0.0 all-gather.2.cloned.1.call-done
  137.0 4.3 %convolution_multiply_fusion = f32[64,1024]{1,0:T(8,128)} fusion(bf16[1024,2048]{1,0:T(8,128)(2,1)} %all-gather.2.cloned.1.call-done, bf16[16,64,128]{2,1,0:T(8,128)(2,1)S(1)} %all-to-all-done.4), kind=kOutput, calls=%fused_computation | convolution fusion | flops 268500992 | bytes 4718592 | tf_op jit(solution)/shard_map/dot_general | solution.py:375
Async XLA Ops:
  7.2 36.3 %copy-start = (bf16[1024,1024]{1,0:T(8,128)(2,1)S(1)}, bf16[1024,1024]{1,0:T(8,128)(2,1)}, u32[]{:S(2)}) copy-start(bf16[1024,1024]{1,0:T(8,128)(2,1)} %param.16) | copy-start | bytes 6291460
  7.2 129.8 %all-gather.2.cloned.1.call-start = ((), (), s32[]{:S(2)}) async-start(), calls=%async_computation.5 | async-start | bytes 4456448 | tf_op jit(solution)/shard_map/all_gather | solution.py:290
  9.6 27.8 %all-to-all-start.1 = ((bf16[64,16,128]{2,0,1:T(8,128)(2,1)}), bf16[64,16,128]{2,0,1:T(8,128)(2,1)S(1)}, u32[]{:S(2)}, u32[]{:S(2)}) async-start(bf16[64,16,128]{2,0,1:T(8,128)(2,1)} %copy_bitcast_fusion.1), calls=%async_computation.1 | async-start | bytes 524288 | tf_op jit(solution)/shard_map/all_to_all | solution.py:291
  37.4 37.5 %all-to-all-start = ((f32[16,96,128]{2,1,0:T(8,128)}), f32[16,96,128]{2,1,0:T(8,128)S(1)}, u32[]{:S(2)}, u32[]{:S(2)}) async-start(f32[16,96,128]{2,1,0:T(8,128)} %get-tuple-element.30), calls=%async_computation | async-start | bytes 1572864 | tf_op jit(solution)/shard_map/all_to_all | solution.py:319
  74.9 17.0 %copy-start.1 = (f32[16,96,128]{2,1,0:T(8,128)}, f32[16,96,128]{2,1,0:T(8,128)S(1)}, u32[]{:S(2)}) copy-start(f32[16,96,128]{2,1,0:T(8,128)S(1)} %all-to-all-done.pay_ref) | copy-start | bytes 2359300
  74.9 17.0 %all-to-all-start.2 = ((f32[16,32,128]{2,1,0:T(8,128)}), f32[16,32,128]{2,1,0:T(8,128)}, u32[]{:S(2)}, u32[]{:S(2)}) async-start(f32[16,32,128]{2,1,0:T(8,128)} %get-tuple-element.42), calls=%async_computation.2 | async-start | bytes 524288 | tf_op jit(solution)/shard_map/all_to_all | solution.py:335
  119.8 17.1 %all-to-all-start.4 = ((bf16[16,64,128]{2,1,0:T(8,128)(2,1)}), bf16[16,64,128]{2,1,0:T(8,128)(2,1)S(1)}, u32[]{:S(2)}, u32[]{:S(2)}) async-start(bf16[16,64,128]{2,1,0:T(8,128)(2,1)} %bitcast.27), calls=%async_computation.4 | async-start | bytes 524288 | tf_op jit(solution)/shard_map/all_to_all | solution.py:361
Sparse Core Ops, SparseCore 0:
  10.1 68.4 all-gather.1

commit v3 on v2

--- a/solution.py
+++ b/solution.py
@@ -211,24 +211,75 @@
             pay_ref[to] = pull[part * rows_each : (part + 1) * rows_each]
 
 
-def relay_kernel(rows_each, pay_ref, pull_ref, start_ref, out_ref):
-    count = pay_ref.shape[0]
+def relay_kernel(rows_each, count, pay_ref, pull_ref, start_ref, state_out, grad_out,
+                 held, local_sem, send_sem, recv_sem):
+    me = lax.axis_index("tm")
     diagonal = (iota((PAIR, PAIR), 0) // HEAD_SIZE) == (iota((PAIR, PAIR), 1) // HEAD_SIZE)
+    outs = (state_out, grad_out)
+    barrier = pltpu.get_barrier_semaphore()
+
+    def greet(i, carried):
+        @pl.when(i != me)
+        def _():
+            pl.semaphore_signal(
+                barrier, inc=1, device_id={"tm": i}, device_id_type=pl.DeviceIdType.MESH
+            )
+
+        return carried
+
+    lax.fori_loop(0, count, greet, 0)
+    pl.semaphore_wait(barrier, count - 1)
+
+    def rows(i):
+        return pl.ds(pl.multiple_of(i * rows_each, rows_each), rows_each)
+
+    def remote(way, i, origin):
+        return pltpu.make_async_remote_copy(
+            src_ref=held.at[way, i],
+            dst_ref=outs[way].at[rows(origin)],
+            send_sem=send_sem.at[way, i],
+            recv_sem=recv_sem.at[way, origin],
+            device_id={"tm": i},
+            device_id_type=pl.DeviceIdType.MESH,
+        )
+
+    def own(way):
+        return pltpu.make_async_copy(held.at[way, me], outs[way].at[rows(me)], local_sem.at[way])
+
+    def send(way, i):
+        @pl.when(i != me)
+        def _():
+            remote(way, i, me).start()
+
+        @pl.when(i == me)
+        def _():
+            own(way).start()
 
     def lap(i, carried):
         state, grad = carried
         j = count - 1 - i
-        out_ref[i, :rows_each] = state
-        out_ref[j, rows_each:] = grad
-        state = pay_ref[i, HEAD_SIZE:] + dot3(
-            state, unpack(pay_ref[i, :HEAD_SIZE], diagonal), NN
-        )
-        grad = pull_ref[j] + dot3(
-            grad, unpack(pay_ref[j, :HEAD_SIZE], diagonal), NT
-        )
+        held[0, i] = state
+        held[1, j] = grad
+        state = pay_ref[i, HEAD_SIZE:] + dot3(state, unpack(pay_ref[i, :HEAD_SIZE], diagonal), NN)
+        grad = pull_ref[j] + dot3(grad, unpack(pay_ref[j, :HEAD_SIZE], diagonal), NT)
+        send(0, i)
+        send(1, j)
         return state, grad
 
     lax.fori_loop(0, count, lap, (start_ref[...], jnp.zeros((rows_each, PAIR), F32)))
+
+    def finish(i, carried):
+        @pl.when(i != me)
+        def _():
+            for way in range(2):
+                remote(way, i, me).wait_send()
+                remote(way, i, i).wait_recv()
+
+        return carried
+
+    lax.fori_loop(0, count, finish, 0)
+    own(0).wait()
+    own(1).wait()
 
 
 def output_kernel(state_ref, y_ref, yr_ref, ylow_ref):
@@ -337,15 +388,27 @@
     start = lax.dynamic_slice_in_dim(
         start.reshape(PAIRS * HEAD_SIZE, PAIR), lax.axis_index("tm") * rows_each, rows_each, 0
     )
-    entries = pl.pallas_call(
-        functools.partial(relay_kernel, rows_each),
-        out_shape=jax.ShapeDtypeStruct((size, 2 * rows_each, PAIR), F32),
-        compiler_params=params,
+    whole = pl.BlockSpec(memory_space=pltpu.VMEM)
+    anywhere = pl.BlockSpec(memory_space=pl.ANY)
+    landed = jax.ShapeDtypeStruct((PAIRS * HEAD_SIZE, PAIR), F32)
+    state, grad = pl.pallas_call(
+        functools.partial(relay_kernel, rows_each, size),
+        in_specs=[whole] * 3,
+        out_specs=[anywhere] * 2,
+        out_shape=[landed] * 2,
+        scratch_shapes=[
+            pltpu.VMEM((2, size, rows_each, PAIR), F32),
+            pltpu.SemaphoreType.DMA((2,)),
+            pltpu.SemaphoreType.DMA((2, size)),
+            pltpu.SemaphoreType.DMA((2, size)),
+        ],
+        compiler_params=pltpu.CompilerParams(
+            collective_id=0, has_side_effects=True, vmem_limit_bytes=32 << 20
+        ),
         name="relay",
     )(arrived, pull, start)
-    entries = lax.all_to_all(entries, "tm", split_axis=0, concat_axis=0, tiled=True)
-    state = entries[:, :rows_each].reshape(PAIRS, HEAD_SIZE, PAIR)
-    grad = entries[:, rows_each:].reshape(PAIRS, HEAD_SIZE, PAIR)
+    state = state.reshape(PAIRS, HEAD_SIZE, PAIR)
+    grad = grad.reshape(PAIRS, HEAD_SIZE, PAIR)
     small = pl.BlockSpec((group, HEAD_SIZE, PAIR), lambda i: (i, 0, 0))
     y_low = pl.pallas_call(
         output_kernel,

time: 149 us -> 143 us (0.960)
  blocking collectives: 17.8 us -> 0 us
  Pallas kernels: 58.3 us -> 70.1 us
    all_to_all x1 -> x0, blocking collectives: 17.8 us -> none  [local(): lax.all_to_all(entries, 'tm', split_axis=0, concat_axis=0, tiled=True)]
    pallas_call x1, Pallas kernels: 5.24 us -> 17 us  [local(): pl.pallas_call(functools.partial(relay_kernel, rows_each, size), in_specs...]
  transfers between devices with their start and end apart: 5 -> 5, of which waited for: 2 -> 2; matrix products, arithmetic and copies ran while one was open for 5% -> 5% of each run, Pallas kernels for 39% -> 49%
where the time goes in v3:
time: 143 us; the launch traced here: 142 us
  Pallas kernels  70.1 us (49%)
  starting transfers between devices  23.9 us (17%)
  waiting for transfers between devices  21.2 us (15%)
  between operations  14.2 us (10%)
  local copies, waits for them, and re-layouts  6.73 us (5%)
  matrix products  5.9 us (4%)
    pallas_call x1, Pallas kernels, local(): pl.pallas_call(functools.partial(forward_kernel, rows_each), grid=steps,...  20.3 us
    pallas_call x1, Pallas kernels, local(): pl.pallas_call(functools.partial(relay_kernel, rows_each, size), in_specs...  17 us
    pallas_call x1, Pallas kernels, local(): pl.pallas_call(functools.partial(backward_kernel, rows_each), grid=steps,...  15.7 us
    all_to_all x1, waiting for transfers between devices, local(): lax.all_to_all(payload, 'tm', split_axis=0, concat_axis=0, tiled=True)  14.1 us
    pallas_call x1, Pallas kernels, local(): pl.pallas_call(last_kernel, grid=steps, in_specs=[small, small] + [block]...  13 us
    all_to_all x1, starting transfers between devices, local(): lax.all_to_all(grad_output, 'tm', split_axis=1, concat_axis=0, tiled=True)  7.41 us
    all_to_all x1, starting transfers between devices, local(): pull = lax.all_to_all(pull, 'tm', split_axis=0, concat_axis=0, tiled=True)  6.94 us
    all_to_all x1, waiting for transfers between devices, local(): pull = lax.all_to_all(pull, 'tm', split_axis=0, concat_axis=0, tiled=True)  6.4 us
  transfers between devices with their start and end apart: 5, of which 2 were waited for; matrix products, arithmetic and copies ran while one was open for 5% of the time, Pallas kernels for 49%

profile of v3, /device:TPU:0, one launch (start us, length us, event | category | flops | bytes accessed | tf_op | source)
XLA Modules:
  0.0 142.0 jit_solution(15242160489501273072)
XLA Ops:
  7.2 0.0 copy-start
  7.2 0.0 all-gather.2.cloned.1.call-start
  7.2 0.7 all-gather.2.cloned.1.call-update
  7.9 1.7 %copy_bitcast_fusion.1 = bf16[64,16,128]{2,0,1:T(8,128)(2,1)} fusion(bf16[64,2048]{1,0:T(8,128)(2,1)} %param.17), kind=kLoop, calls=%fused_computation.4 | loop fusion | bytes 524288 | tf_op jit(solution)/shard_map/all_to_all | solution.py:342
  9.6 7.4 %all-to-all-start.1 = ((bf16[64,16,128]{2,0,1:T(8,128)(2,1)}), bf16[64,16,128]{2,0,1:T(8,128)(2,1)S(1)}, u32[]{:S(2)}, u32[]{:S(2)}) async-start(bf16[64,16,128]{2,0,1:T(8,128)(2,1)} %copy_bitcast_fusion.1), calls=%async_computation.1 | async-start | bytes 524288 | tf_op jit(solution)/shard_map/all_to_all | solution.py:342
  17.1 20.3 %forward.1 = (f32[16,96,128]{2,1,0:T(8,128)}, f32[128,1024]{1,0:T(8,128)}, f32[128,1024]{1,0:T(8,128)}, f32[128,1024]{1,0:T(8,128)}, f32[128,1024]{1,0:T(8,128)}...) custom-call(bf16[128,1024]{1,0:T(8,128)(2,1)} %rec_ref.3, ...), custom_call_target="tpu_custom_call" | custom-call | flops 21474836480 | bytes 10485760 | tf_op jit(solution)/shard_map/forward/pallas_call | solution.py:360
  37.4 0.0 all-to-all-done.1
  37.4 6.0 %all-to-all-start = ((f32[16,96,128]{2,1,0:T(8,128)}), f32[16,96,128]{2,1,0:T(8,128)S(1)}, u32[]{:S(2)}, u32[]{:S(2)}) async-start(f32[16,96,128]{2,1,0:T(8,128)} %get-tuple-element.32), calls=%async_computation | async-start | bytes 1572864 | tf_op jit(solution)/shard_map/all_to_all | solution.py:370
  43.4 0.0 copy-done
  43.4 1.6 %fusion.2.gy_ref = f32[128,1024]{1,0:T(8,128)} fusion(bf16[1024,128]{1,0:T(8,128)(2,1)S(1)} %bitcast.31, bf16[1024,1024]{1,0:T(8,128)(2,1)S(1)} %copy-done), kind=kOutput, calls=%fused_computation.6 | convolution fusion | flops 268435456 | bytes 2883584 | tf_op jit(solution)/shard_map/dot_general | solution.py:371
  45.0 15.7 %backward.1 = (f32[16,32,128]{2,1,0:T(8,128)}, f32[128,1024]{1,0:T(8,128)}, f32[128,1024]{1,0:T(8,128)}, f32[128,1024]{1,0:T(8,128)}, f32[128,1024]{1,0:T(8,128)...) custom-call(bf16[128,1024]{1,0:T(8,128)(2,1)} %rec_ref.3, bf16[128,1024]{1,0:T(8,128)(2,1)} %val_ref.5, ...), custom_call_target="tpu_custom_call" | custom-call | flops 12884901888 | bytes 10485760 | tf_op jit(solution)/shard_map/backward/pallas_call | solution.py:375
  60.8 14.1 %all-to-all-done.pay_ref = f32[16,96,128]{2,1,0:T(8,128)S(1)} async-done(((f32[16,96,128]{2,1,0:T(8,128)}), f32[16,96,128]{2,1,0:T(8,128)S(1)}, u32[]{:S(2)}, u32[]{:S(2)}) %all-to-all-start) | async-done | bytes 786464 | tf_op jit(solution)/shard_map/all_to_all | solution.py:370
  74.9 6.9 %all-to-all-start.2 = ((f32[16,32,128]{2,1,0:T(8,128)}), f32[16,32,128]{2,1,0:T(8,128)S(1)}, u32[]{:S(2)}, u32[]{:S(2)}) async-start(f32[16,32,128]{2,1,0:T(8,128)} %get-tuple-element.44), calls=%async_computation.2 | async-start | bytes 524288 | tf_op jit(solution)/shard_map/all_to_all | solution.py:386
  81.9 2.2 %copy.30 = f32[8,2,64,64]{3,1,2,0:T(2,128)} copy(f32[8,2,64,64]{3,2,1,0:T(8,128)} %bitcast.32) | data formatting | bytes 524288 | tf_op jit(solution)/shard_map/reshape | solution.py:387
  84.1 1.3 reshape.30
  85.5 6.4 %all-to-all-done.2.pull_ref = f32[16,32,128]{2,1,0:T(8,128)S(1)} async-done(((f32[16,32,128]{2,1,0:T(8,128)}), f32[16,32,128]{2,1,0:T(8,128)S(1)}, u32[]{:S(2)}, u32[]{:S(2)}) %all-to-all-start.2) | async-done | bytes 262176 | tf_op jit(solution)/shard_map/all_to_all | solution.py:386
  91.9 17.0 %relay.1 = (f32[512,128]{1,0:T(8,128)S(1)}, f32[512,128]{1,0:T(8,128)S(1)}) custom-call(f32[16,96,128]{2,1,0:T(8,128)S(1)} %all-to-all-done.pay_ref, f32[16,32,128]{2,1,0:T(8,128)S(1)} %all-to-all-done.2.pull_ref, f32[32,128]{1,0:T(8,128)S(1)} %constant_dynamic-slice_fusion.start_ref), custom_call_target="tpu_custom_call" | custom-call | tf_op jit(solution)/shard_map/relay/pallas_call | solution.py:394
  108.9 0.0 copy-start.1
  108.9 0.7 copy-done.1
  109.6 0.0 copy-start.2
  109.6 0.7 copy-done.2
  110.3 4.0 %output.1 = bf16[1024,128]{1,0:T(8,128)(2,1)} custom-call(f32[8,64,128]{2,1,0:T(8,128)} %bitcast.26, f32[128,1024]{1,0:T(8,128)} %get-tuple-element.58.y_ref, f32[128,1024]{1,0:T(8,128)} %get-tuple-element.59.yr_ref), custom_call_target="tpu_custom_call" | custom-call | flops 268435456 | bytes 2097152 | tf_op jit(solution)/shard_map/output/pallas_call | solution.py:413
  114.3 3.5 %all-to-all-start.3 = ((bf16[16,64,128]{2,1,0:T(8,128)(2,1)}), bf16[16,64,128]{2,1,0:T(8,128)(2,1)S(1)}, u32[]{:S(2)}, u32[]{:S(2)}) async-start(bf16[16,64,128]{2,1,0:T(8,128)(2,1)} %bitcast.30), calls=%async_computation.3 | async-start | bytes 524288 | tf_op jit(solution)/shard_map/all_to_all | solution.py:424
  117.9 13.0 %last.1 = (bf16[128,1024]{1,0:T(8,128)(2,1)}, bf16[128,1024]{1,0:T(8,128)(2,1)}, bf16[128,1024]{1,0:T(8,128)(2,1)}) custom-call(f32[8,64,128]{2,1,0:T(8,128)} %bitcast.27, f32[8,64,128]{2,1,0:T(8,128)} %bitcast.28, f32[128,1024]{1,0:T(8,128)} %fusion.2.gy_ref, bf16[128,1024]{1,0:T(8,128)(2,1)} %val_ref.5, f32[128,1024]{1,0:T(8,128)} %get-tuple-element.47.u_ref, ...), custom_call_target="tpu_custom_call" | custom-call | flops 8589934592 | bytes 8388608 | tf_op jit(solution)/shard_map/last/pallas_call | solution.py:425
  130.9 0.0 all-to-all-done.3
  130.9 0.0 all-gather.2.cloned.1.call-done
  130.9 4.3 %convolution_multiply_fusion = f32[64,1024]{1,0:T(8,128)} fusion(bf16[1024,2048]{1,0:T(8,128)(2,1)} %all-gather.2.cloned.1.call-done, bf16[16,64,128]{2,1,0:T(8,128)(2,1)S(1)} %all-to-all-done.3), kind=kOutput, calls=%fused_computation | convolution fusion | flops 268500992 | bytes 4718592 | tf_op jit(solution)/shard_map/dot_general | solution.py:438
  (1 shorter events, 0.0 us)
Async XLA Ops:
  7.2 36.2 %copy-start = (bf16[1024,1024]{1,0:T(8,128)(2,1)S(1)}, bf16[1024,1024]{1,0:T(8,128)(2,1)}, u32[]{:S(2)}) copy-start(bf16[1024,1024]{1,0:T(8,128)(2,1)} %param.16) | copy-start | bytes 6291460
  7.2 123.7 %all-gather.2.cloned.1.call-start = ((), (), s32[]{:S(2)}) async-start(), calls=%async_computation.4 | async-start | bytes 4456448 | tf_op jit(solution)/shard_map/all_gather | solution.py:341
  9.6 27.8 %all-to-all-start.1 = ((bf16[64,16,128]{2,0,1:T(8,128)(2,1)}), bf16[64,16,128]{2,0,1:T(8,128)(2,1)S(1)}, u32[]{:S(2)}, u32[]{:S(2)}) async-start(bf16[64,16,128]{2,0,1:T(8,128)(2,1)} %copy_bitcast_fusion.1), calls=%async_computation.1 | async-start | bytes 524288 | tf_op jit(solution)/shard_map/all_to_all | solution.py:342
  37.4 37.5 %all-to-all-start = ((f32[16,96,128]{2,1,0:T(8,128)}), f32[16,96,128]{2,1,0:T(8,128)S(1)}, u32[]{:S(2)}, u32[]{:S(2)}) async-start(f32[16,96,128]{2,1,0:T(8,128)} %get-tuple-element.32), calls=%async_computation | async-start | bytes 1572864 | tf_op jit(solution)/shard_map/all_to_all | solution.py:370
  74.9 17.0 %all-to-all-start.2 = ((f32[16,32,128]{2,1,0:T(8,128)}), f32[16,32,128]{2,1,0:T(8,128)S(1)}, u32[]{:S(2)}, u32[]{:S(2)}) async-start(f32[16,32,128]{2,1,0:T(8,128)} %get-tuple-element.44), calls=%async_computation.2 | async-start | bytes 524288 | tf_op jit(solution)/shard_map/all_to_all | solution.py:386
  108.9 0.7 copy-start.1
  109.6 0.7 copy-start.2
  114.3 16.5 %all-to-all-start.3 = ((bf16[16,64,128]{2,1,0:T(8,128)(2,1)}), bf16[16,64,128]{2,1,0:T(8,128)(2,1)S(1)}, u32[]{:S(2)}, u32[]{:S(2)}) async-start(bf16[16,64,128]{2,1,0:T(8,128)(2,1)} %bitcast.30), calls=%async_computation.3 | async-start | bytes 524288 | tf_op jit(solution)/shard_map/all_to_all | solution.py:424
Sparse Core Ops, SparseCore 0:
  10.1 68.4 all-gather.1
